TPU v7x, 32 devices: a whole 2x2x4 slice. The times are simulated.
32 devices in a mesh: cuts: 8 (over z, core), row: 4 (over y, x).
Axes of the slice: x: 2, y: 2, z: 4, core: 2. Of those that a mesh axis runs over, the one named last changes fastest.
Arguments:
- field: float32 [2, 64, 256, 256], P(None, 'cuts', 'row'), may hold values from -6 to 6
- row_prop: float32 [2, 256, 256], replicated, may hold values from -0.25 to 0.25
- col_prop: float32 [2, 256, 256], replicated, may hold values from -0.25 to 0.25
- phase: float32 [64, 8192], P('cuts', 'row'), may hold values from -3.140625 to 3.140625
- energy: float32 [64, 8192], P('cuts', 'row'), may hold values from -6 to 6
- cells: int32 [64, 8192], P('cuts', 'row'), may hold values from 0 to 65535, as said below
- shifts: int32 [4], replicated, may hold values from 1 to 2, as said below
Outputs:
- field_out: float32 [2, 64, 256, 256], P(None, 'cuts', 'row')
- phase_out: float32 [64, 8192], P('cuts', 'row')
- energy_out: float32 [64, 8192], P('cuts', 'row')
- bunching: float32 [4, 2, 64], P(None, None, 'cuts')
Inputs may be any that keep to these rules, and one draw needn't show every extreme that they name: `cells`: electron j of a slice sits in a grid row from b * 64 to (b + 1) * 64 - 1, where b = j // 2048. `shifts`: 2 slices slip in at least one period.
All inputs are finite; a program needn't handle non-finite values.
Results may differ from a plain program's by a relative error of at most 0.00021.
Values sent between devices are 32-bit elements; how exact they have to be, the bound alone decides.
No kernel may reach another device: no remote copies, remote signals or barrier semaphores. Data moves between devices by JAX's collectives and lax.ppermute only.
A program may use at most 64 MiB of HBM per device.

v0:
```python
import jax
import jax.numpy as jnp
from jax import lax
from jax.sharding import PartitionSpec as P

ELEC = 8192
PERIODS = 4
KMAX = 2


kick_rate = 0.5
source_gain = 0.5


def shifted(value, axis, steps):
    count = lax.axis_size(axis)
    initial, last = (max(0, -steps), min(count, count - steps))
    return lax.ppermute(value, axis, [(source, source + steps) for source in range(initial, last)])


def rows_product(matrix, values):
    return jnp.einsum("rk,skc->src", matrix, values, precision=lax.Precision.HIGHEST)


def cols_product(matrix, values):
    return jnp.einsum("ck,srk->src", matrix, values, precision=lax.Precision.HIGHEST)


def complex_rows(prop, values):
    return jnp.stack(
        [
            rows_product(prop[0], values[0]) - rows_product(prop[1], values[1]),
            rows_product(prop[0], values[1]) + rows_product(prop[1], values[0]),
        ]
    )


def shards(field, row_prop, col_prop, phase, energy, cells, shifts):
    count = field.shape[1]
    row_count = field.shape[2]
    col_count = field.shape[3]
    row_start = lax.axis_index("row") * row_count
    local_cells = cells - row_start * col_count
    cell_row = local_cells // col_count
    cell_col = local_cells - cell_row * col_count
    row_pick = (
        cell_row[:, None, :] == jnp.arange(row_count, dtype=jnp.int32)[None, :, None]
    ).astype(jnp.float32)
    col_pick = (
        cell_col[:, :, None] == jnp.arange(col_count, dtype=jnp.int32)[None, None, :]
    ).astype(jnp.float32)
    own_prop = lax.dynamic_slice_in_dim(row_prop, row_start, row_count, 1)
    partials = []
    for period in range(PERIODS):
        last_slices = field[:, count - KMAX :]
        arrived = shifted(last_slices, "cuts", 1)
        joined = jnp.concatenate([arrived, field], axis=1)
        field = lax.dynamic_slice_in_dim(joined, KMAX - shifts[period], count, 1)
        by_column = jnp.einsum("psrc,sec->psre", field, col_pick, precision=lax.Precision.HIGHEST)
        samples = jnp.sum(by_column * row_pick[None], axis=2)
        sample_real = samples[0]
        sample_imag = samples[1]
        energy = energy - kick_rate * (sample_real * jnp.cos(phase) - sample_imag * jnp.sin(phase))
        phase = phase + energy
        emit_real = jnp.cos(phase)
        emit_imag = -jnp.sin(phase)
        local_sums = jnp.stack([jnp.sum(emit_real, 1), jnp.sum(emit_imag, 1)])
        partials.append(lax.psum(local_sums, "row"))
        emitted = jnp.stack([emit_real, emit_imag])
        weighted = row_pick[None] * emitted[:, :, None, :]
        deposit = jnp.einsum("psre,sec->psrc", weighted, col_pick, precision=lax.Precision.HIGHEST)
        field = field + source_gain * deposit
        field = jnp.stack(
            [
                cols_product(col_prop[0], field[0]) - cols_product(col_prop[1], field[1]),
                cols_product(col_prop[0], field[1]) + cols_product(col_prop[1], field[0]),
            ]
        )
        field = complex_rows(own_prop, lax.all_gather(field, "row", axis=2, tiled=True))
    bunching = jnp.stack(partials)
    bunching = bunching * ELEC ** (-0.5)
    return (field, phase, energy, bunching)


def solution(mesh):
    return jax.shard_map(
        shards,
        mesh=mesh,
        in_specs=(
            P(None, "cuts", "row", None),
            P(),
            P(),
            P("cuts", "row"),
            P("cuts", "row"),
            P("cuts", "row"),
            P(),
        ),
        out_specs=(
            P(None, "cuts", "row", None),
            P("cuts", "row"),
            P("cuts", "row"),
            P(None, None, "cuts"),
        ),
        check_vma=False,
    )
```

profile of v0, /device:TPU:0, one launch (start us, length us, event | category | flops | bytes accessed | tf_op | source)
XLA Modules:
  0.0 394.8 jit_solution(15644956505941779119)
XLA Ops:
  8.4 2.4 collective-permute-start
  11.7 2.5 fusion.41
  16.1 11.8 %fusion.20 = f32[2,8,2048]{2,0,1:T(2,128)S(1)} fusion(f32[8,64,2048]{2,1,0:T(8,128)} %fusion.41, s32[8,2048]{1,0:T(8,128)S(1)} %get-tuple-element.35, s32[]{:T(128)S(6)} %select_n.20, f32[2,2,64,256]{3,2,0,1:T(8,128)S(1)} %collective-permute-done, f32[2,8,64,256]{3,2,1,0:T(8,128)S(1)} %copy-done.13), kind=kOutput, calls=%fused_computation.17 | convolution fusion | flops 6451068928 | bytes 5701636 | tf_op jit(solution)/shard_map/psrc,sec->psre/dot_general | solution.py:59
  28.9 7.0 %fusion.76 = f32[2,8,64,256]{3,2,0,1:T(8,128)S(1)} fusion(f32[2,8,2048]{2,0,1:T(2,128)S(1)} %copy.20, f32[8,64,2048]{2,1,0:T(8,128)S(1)} %copy-done.6, s32[8,2048]{1,0:T(8,128)S(1)} %get-tuple-element.35, s32[]{:T(128)S(6)} %select_n.20, f32[2,2,64,256]{3,2,0,1:T(8,128)S(1)} %collective-permute-done, f32[2,8,64,256]{3,2,1,0:T(8,128)S(1)} %copy-done.13), kind=kOutput, calls=%fused_computation.66 | convolution fusion | flops 6449528832 | bytes 6750212 | tf_op jit(solution)/shard_map/psre,sec->psrc/dot_general | solution.py:71
  39.8 55.1 %all-gather.5.cloned.1.call-done = f32[2,8,256,256]{3,2,1,0:T(8,128)} async-done(((f32[2,8,64,256]{3,2,1,0:T(8,128)}), f32[2,8,256,256]{3,2,1,0:T(8,128)}) %all-gather.5.cloned.1.call-update) | async-done | bytes 4194320 | tf_op jit(solution)/shard_map/all_gather | solution.py:79
  94.9 3.2 fusion.51
  98.1 3.0 fusion.50
  107.2 11.6 %fusion.19 = f32[2,8,2048]{2,0,1:T(2,128)S(1)} fusion(f32[8,64,2048]{2,1,0:T(8,128)} %fusion.41, f32[2,8,64,256]{3,2,0,1:T(8,128)S(1)} %fusion.154, s32[8,2048]{1,0:T(8,128)S(1)} %get-tuple-element.35), kind=kOutput, calls=%fused_computation.15 | convolution fusion | flops 6450806784 | bytes 5439488 | tf_op jit(solution)/shard_map/psrc,sec->psre/dot_general | solution.py:59
  119.9 8.1 %fusion.91 = f32[2,8,64,256]{3,2,0,1:T(8,128)S(1)} fusion(f32[2,8,64,256]{3,2,0,1:T(8,128)S(1)} %fusion.154, f32[2,8,2048]{2,0,1:T(2,128)S(1)} %copy.23, f32[8,64,2048]{2,1,0:T(8,128)S(1)} %copy-done.7, s32[8,2048]{1,0:T(8,128)S(1)} %get-tuple-element.35), kind=kOutput, calls=%fused_computation.69 | convolution fusion | flops 6449266688 | bytes 6488064 | tf_op jit(solution)/shard_map/psre,sec->psrc/dot_general | solution.py:71
  132.1 56.9 %all-gather.7.cloned.1.call-done = f32[2,8,256,256]{3,2,1,0:T(8,128)} async-done(((f32[2,8,64,256]{3,2,1,0:T(8,128)}), f32[2,8,256,256]{3,2,1,0:T(8,128)}) %all-gather.7.cloned.1.call-update) | async-done | bytes 4194320 | tf_op jit(solution)/shard_map/all_gather | solution.py:79
  189.1 3.2 fusion.54
  192.3 3.0 fusion.55
  201.3 11.6 %fusion.18 = f32[2,8,2048]{2,0,1:T(2,128)S(1)} fusion(f32[8,64,2048]{2,1,0:T(8,128)} %fusion.41, f32[2,8,64,256]{3,2,0,1:T(8,128)S(1)} %fusion.152, s32[8,2048]{1,0:T(8,128)S(1)} %get-tuple-element.35), kind=kOutput, calls=%fused_computation.13 | convolution fusion | flops 6450806784 | bytes 5439488 | tf_op jit(solution)/shard_map/psrc,sec->psre/dot_general | solution.py:59
  213.8 8.1 %fusion.106 = f32[2,8,64,256]{3,2,0,1:T(8,128)S(1)} fusion(f32[2,8,64,256]{3,2,0,1:T(8,128)S(1)} %fusion.152, f32[2,8,2048]{2,0,1:T(2,128)S(1)} %copy.26, f32[8,64,2048]{2,1,0:T(8,128)S(1)} %copy-done.8, s32[8,2048]{1,0:T(8,128)S(1)} %get-tuple-element.35), kind=kOutput, calls=%fused_computation.72 | convolution fusion | flops 6449266688 | bytes 6488064 | tf_op jit(solution)/shard_map/psre,sec->psrc/dot_general | solution.py:71
  225.8 57.3 %all-gather.9.cloned.1.call-done = f32[2,8,256,256]{3,2,1,0:T(8,128)} async-done(((f32[2,8,64,256]{3,2,1,0:T(8,128)}), f32[2,8,256,256]{3,2,1,0:T(8,128)}) %all-gather.9.cloned.1.call-update) | async-done | bytes 4194320 | tf_op jit(solution)/shard_map/all_gather | solution.py:79
  283.1 3.2 fusion.58
  286.3 3.0 fusion.59
  292.3 1.6 collective-permute-start.3
  295.3 11.6 %fusion.17 = f32[2,8,2048]{2,0,1:T(2,128)S(1)} fusion(f32[8,64,2048]{2,1,0:T(8,128)} %fusion.41, f32[2,8,64,256]{3,2,0,1:T(8,128)S(1)} %fusion.150, s32[8,2048]{1,0:T(8,128)S(1)} %get-tuple-element.35), kind=kOutput, calls=%fused_computation.11 | convolution fusion | flops 6450806784 | bytes 5439488 | tf_op jit(solution)/shard_map/psrc,sec->psre/dot_general | solution.py:59
  308.6 8.1 %fusion.121 = f32[2,8,64,256]{3,2,0,1:T(8,128)S(1)} fusion(f32[2,8,64,256]{3,2,0,1:T(8,128)S(1)} %fusion.150, f32[2,8,2048]{2,0,1:T(2,128)S(1)} %copy.29, f32[8,64,2048]{2,1,0:T(8,128)S(1)} %copy-done.9, s32[8,2048]{1,0:T(8,128)S(1)} %get-tuple-element.35), kind=kOutput, calls=%fused_computation.75 | convolution fusion | flops 6449266688 | bytes 6488064 | tf_op jit(solution)/shard_map/psre,sec->psrc/dot_general | solution.py:71
  320.5 9.1 %all-reduce = (f32[1,2,8]{2,1,0:T(2,128)S(1)}, f32[1,2,8]{2,1,0:T(2,128)S(1)}, f32[1,2,8]{2,1,0:T(2,128)S(1)}, f32[1,2,8]{2,1,0:T(2,128)S(1)}) all-reduce(f32[1,2,8]{2,1,0:T(2,128)S(1)} %get-tuple-element.44, f32[1,2,8]{2,1,0:T(2,128)S(1)} %get-tuple-element.43, ...), channel_id=1, replica_groups=mesh['cuts'=8,'row'=4] {'row'}, use_global_device_ids=true, to_apply=%region_15.16 | all-reduce | flops 64 | bytes 512 | tf_op jit(solution)/shard_map/psum | solution.py:68
  330.2 47.5 %all-gather.11.cloned.1.call-done = f32[2,8,256,256]{3,2,1,0:T(8,128)} async-done(((f32[2,8,64,256]{3,2,1,0:T(8,128)}), f32[2,8,256,256]{3,2,1,0:T(8,128)}) %all-gather.11.cloned.1.call-update) | async-done | bytes 4194320 | tf_op jit(solution)/shard_map/all_gather | solution.py:79
  377.8 3.2 fusion.62
  381.0 3.0 fusion.63
  (114 shorter events, 39.5 us)
Async XLA Ops:
  7.2 87.7 %copy-start = (f32[2,256,256]{2,1,0:T(8,128)S(1)}, f32[2,256,256]{2,1,0:T(8,128)}, u32[]{:S(2)}) copy-start(f32[2,256,256]{2,1,0:T(8,128)} %param.8) | copy-start | bytes 1572868
  7.2 8.9 %copy-start.13 = (f32[2,8,64,256]{3,2,1,0:T(8,128)S(1)}, f32[2,8,64,256]{3,2,1,0:T(8,128)}, u32[]{:S(2)}) copy-start(f32[2,8,64,256]{3,2,1,0:T(8,128)} %param.7) | copy-start | bytes 3145732
  7.2 6.9 %copy-start.14 = (s32[4]{0:T(128)S(1)}, s32[4]{0:T(128)}, u32[]{:S(2)}) copy-start(s32[4]{0:T(128)} %param.13) | copy-start | bytes 52
  7.2 87.7 %all-gather.5.cloned.1.call-start = ((), (), s32[]{:S(2)}) async-start(), calls=%async_computation | async-start | bytes 5242880 | tf_op jit(solution)/shard_map/all_gather | solution.py:79
  8.4 7.7 %collective-permute-start = (f32[2,2,64,256]{3,2,0,1:T(8,128)S(1)}, f32[2,2,64,256]{3,2,0,1:T(8,128)S(1)}, u32[]{:S(2)}, u32[]{:S(2)}) collective-permute-start(f32[2,2,64,256]{3,2,0,1:T(8,128)S(1)} %copy.114), channel_id=1, source_target_pairs={{0,4},{4,8},{8,12},{12,16},{16,20},{20,24},{24,28},{1,5},{5,9},{9,... | collective-permute-start | bytes 786440 | tf_op jit(solution)/shard_map/ppermute | solution.py:18
  16.1 11.9 %copy-start.11 = (f32[8,2048]{1,0:T(8,128)S(1)}, f32[8,2048]{1,0:T(8,128)}, u32[]{:S(2)}) copy-start(f32[8,2048]{1,0:T(8,128)} %param.10) | copy-start | bytes 196612
  16.1 11.9 %copy-start.12 = (f32[8,2048]{1,0:T(8,128)S(1)}, f32[8,2048]{1,0:T(8,128)}, u32[]{:S(2)}) copy-start(f32[8,2048]{1,0:T(8,128)} %param.11) | copy-start | bytes 196612
  16.1 12.8 %copy-start.6 = (f32[8,64,2048]{2,1,0:T(8,128)S(1)}, f32[8,64,2048]{2,1,0:T(8,128)}, u32[]{:S(2)}) copy-start(f32[8,64,2048]{2,1,0:T(8,128)} %fusion.41) | copy-start | bytes 12582916
  28.9 7.0 %copy-start.1 = (f32[2,256,256]{2,1,0:T(8,128)S(1)}, f32[2,256,256]{2,1,0:T(8,128)}, u32[]{:S(2)}) copy-start(f32[2,256,256]{2,1,0:T(8,128)} %param.9) | copy-start | bytes 1572868
  39.5 149.6 %all-gather.7.cloned.1.call-start = ((), (), s32[]{:S(2)}) async-start(), calls=%async_computation.1 | async-start | bytes 5242880 | tf_op jit(solution)/shard_map/all_gather | solution.py:79
  94.9 6.2 %copy-start.3 = (f32[2,8,256,256]{3,2,1,0:T(8,128)S(1)}, f32[2,8,256,256]{3,2,1,0:T(8,128)}, u32[]{:S(2)}) copy-start(f32[2,8,256,256]{3,2,1,0:T(8,128)} %all-gather.5.cloned.1.call-done) | copy-start | bytes 12582916
  104.1 2.9 collective-permute-start.1
  107.2 12.7 %copy-start.7 = (f32[8,64,2048]{2,1,0:T(8,128)S(1)}, f32[8,64,2048]{2,1,0:T(8,128)}, u32[]{:S(2)}) copy-start(f32[8,64,2048]{2,1,0:T(8,128)} %fusion.41) | copy-start | bytes 12582916
  131.6 151.5 %all-gather.9.cloned.1.call-start = ((), (), s32[]{:S(2)}) async-start(), calls=%async_computation.2 | async-start | bytes 5242880 | tf_op jit(solution)/shard_map/all_gather | solution.py:79
  189.1 6.2 %copy-start.4 = (f32[2,8,256,256]{3,2,1,0:T(8,128)S(1)}, f32[2,8,256,256]{3,2,1,0:T(8,128)}, u32[]{:S(2)}) copy-start(f32[2,8,256,256]{3,2,1,0:T(8,128)} %all-gather.7.cloned.1.call-done) | copy-start | bytes 12582916
  198.3 2.9 collective-permute-start.2
  201.3 12.5 %copy-start.8 = (f32[8,64,2048]{2,1,0:T(8,128)S(1)}, f32[8,64,2048]{2,1,0:T(8,128)}, u32[]{:S(2)}) copy-start(f32[8,64,2048]{2,1,0:T(8,128)} %fusion.41) | copy-start | bytes 12582916
  225.5 152.3 %all-gather.11.cloned.1.call-start = ((), (), s32[]{:S(2)}) async-start(), calls=%async_computation.3 | async-start | bytes 5242880 | tf_op jit(solution)/shard_map/all_gather | solution.py:79
  283.1 6.2 %copy-start.5 = (f32[2,8,256,256]{3,2,1,0:T(8,128)S(1)}, f32[2,8,256,256]{3,2,1,0:T(8,128)}, u32[]{:S(2)}) copy-start(f32[2,8,256,256]{3,2,1,0:T(8,128)} %all-gather.9.cloned.1.call-done) | copy-start | bytes 12582916
  292.3 2.9 collective-permute-start.3
  295.3 13.2 %copy-start.9 = (f32[8,64,2048]{2,1,0:T(8,128)S(1)}, f32[8,64,2048]{2,1,0:T(8,128)}, u32[]{:S(2)}) copy-start(f32[8,64,2048]{2,1,0:T(8,128)} %fusion.41) | copy-start | bytes 12582916
  308.1 8.6 %copy-start.10 = (f32[8,2048]{1,0:T(8,128)}, f32[8,2048]{1,0:T(8,128)S(1)}, u32[]{:S(2)}) copy-start(f32[8,2048]{1,0:T(8,128)S(1)} %get-tuple-element.9) | copy-start | bytes 196612
  377.8 6.2 %copy-start.2 = (f32[2,8,256,256]{3,2,1,0:T(8,128)S(1)}, f32[2,8,256,256]{3,2,1,0:T(8,128)}, u32[]{:S(2)}) copy-start(f32[2,8,256,256]{3,2,1,0:T(8,128)} %all-gather.11.cloned.1.call-done) | copy-start | bytes 12582916
Sparse Core Ops, SparseCore 0:
  39.6 55.2 all-gather.4
  131.7 57.3 all-gather.6
  225.7 57.3 all-gather.8
  320.4 57.3 all-gather.10
where the time goes:
time: 402 us; the launch traced here: 395 us
  waiting for transfers between devices  217 us (54%)
  matrix products  125 us (31%)
  between operations  19.8 us (5%)
  other arithmetic  12.6 us (3%)
  blocking collectives  9.15 us (2%)
  starting transfers between devices  8.34 us (2%)
    all_gather x4, waiting for transfers between devices, shards(): lax.all_gather(field, 'row', axis=2, tiled=True)  217 us
    dot_general x4, matrix products, shards(): jnp.einsum('psrc,sec->psre', field, col_pick, precision=lax.Precision.HIG...  46.7 us
    dot_general x16, matrix products, rows_product(): jnp.einsum('rk,skc->src', matrix, values, precision=lax.Precision.HIGHEST)  36.8 us
    dot_general x4, matrix products, shards(): jnp.einsum('psre,sec->psrc', weighted, col_pick, precision=lax.Precision....  31.4 us
    dot_general x16, matrix products, cols_product(): jnp.einsum('ck,srk->src', matrix, values, precision=lax.Precision.HIGHEST)  9.83 us
    psum x1, blocking collectives, shards(): partials.append(lax.psum(local_sums, 'row'))  9.15 us
  transfers between devices with their start and end apart: 8, of which 4 were waited for; matrix products, arithmetic and copies ran while one was open for 1% of the time, Pallas kernels for 0%

commit v1 on v0

--- a/solution.py
+++ b/solution.py
@@ -1,15 +1,17 @@
 import jax
 import jax.numpy as jnp
 from jax import lax
+from jax.experimental import pallas as pl
+from jax.experimental.pallas import tpu as pltpu
 from jax.sharding import PartitionSpec as P
 
-ELEC = 8192
-PERIODS = 4
 KMAX = 2
-
-
 kick_rate = 0.5
 source_gain = 0.5
+BF = jnp.bfloat16
+F32 = jnp.float32
+LANES = 128
+CHUNK = 512
 
 
 def shifted(value, axis, steps):
@@ -35,7 +37,7 @@
     )
 
 
-def shards(field, row_prop, col_prop, phase, energy, cells, shifts):
+def row_blocks(field, row_prop, col_prop, phase, energy, cells, shifts):
     count = field.shape[1]
     row_count = field.shape[2]
     col_count = field.shape[3]
@@ -51,7 +53,7 @@
     ).astype(jnp.float32)
     own_prop = lax.dynamic_slice_in_dim(row_prop, row_start, row_count, 1)
     partials = []
-    for period in range(PERIODS):
+    for period in range(shifts.shape[0]):
         last_slices = field[:, count - KMAX :]
         arrived = shifted(last_slices, "cuts", 1)
         joined = jnp.concatenate([arrived, field], axis=1)
@@ -78,13 +80,478 @@
         )
         field = complex_rows(own_prop, lax.all_gather(field, "row", axis=2, tiled=True))
     bunching = jnp.stack(partials)
-    bunching = bunching * ELEC ** (-0.5)
+    bunching = bunching * (phase.shape[1] * lax.axis_size("row")) ** (-0.5)
     return (field, phase, energy, bunching)
 
 
+def halves(value):
+    high = value.astype(BF)
+    return high, (value - high.astype(F32)).astype(BF)
+
+
+def one_hot(index, size):
+    shape = (size, index.shape[1])
+    level = lax.broadcasted_iota(jnp.int32, shape, 0).astype(BF)
+    return jnp.where(level == jnp.broadcast_to(index.astype(BF), shape), jnp.ones((), BF), jnp.zeros((), BF))
+
+
+def chunks(length):
+    step = CHUNK if length % CHUNK == 0 else length
+    return [(start, step) for start in range(0, length, step)]
+
+
+def vmem_call(kernel, outs, inputs, shifts=None, scratch=()):
+    vmem = pl.BlockSpec(memory_space=pltpu.VMEM)
+    specs = [vmem] * len(inputs)
+    if shifts is not None:
+        specs = [pl.BlockSpec(memory_space=pltpu.SMEM)] + specs
+        inputs = [shifts] + list(inputs)
+    return pl.pallas_call(
+        kernel,
+        out_shape=outs,
+        in_specs=specs,
+        out_specs=jax.tree.map(lambda _: vmem, outs),
+        scratch_shapes=list(scratch),
+        compiler_params=pltpu.CompilerParams(vmem_limit_bytes=48 * 1024 * 1024),
+    )(*inputs)
+
+
+def sds(shape, dtype=F32):
+    return jax.ShapeDtypeStruct(shape, dtype)
+
+
+def remainder(value, divisor):
+    return lax.rem(value + 4 * divisor, jnp.int32(divisor))
+
+
+class Plan:
+    def __init__(self, n_cuts, n_row, field, phase, shifts):
+        self.n_cuts, self.n_row = n_cuts, n_row
+        self.per_cut, self.rows, self.cols = field.shape[1:]
+        self.count = phase.shape[1]
+        self.periods = shifts.shape[0]
+        self.held = max(1, self.per_cut // n_row)
+        self.slots = n_cuts * self.per_cut
+        self.lines = self.held * n_row
+        most, least = KMAX * self.periods, self.periods + 1
+        self.lead = self.held * ((most - KMAX) // self.held)
+        self.ahead = max(0, most - self.lead)
+        self.behind = max(0, self.lead - least)
+        self.turn = self.lead // self.held
+
+    def fits(self):
+        n = self.n_row
+        if n & (n - 1) or self.per_cut % n or self.held < KMAX or self.count % LANES:
+            return False
+        return self.lead < self.per_cut and self.ahead <= self.held and self.behind <= self.held
+
+    def send_pair(self, target):
+        return (target - self.turn) % self.n_row, (self.turn + (target - self.turn) % self.n_row) // self.n_row
+
+    def spread_table(self, d):
+        table = []
+        for c in range(self.n_cuts):
+            for r in range(self.n_row):
+                cuts_on = self.send_pair(r ^ d)[1]
+                table.append((c * self.n_row + r, ((c + cuts_on) % self.n_cuts) * self.n_row + (r ^ d)))
+        return table
+
+
+def split_cells(cells, block, rows, cols):
+    flat = cells.astype(jnp.int32)
+    row = lax.div(flat, jnp.int32(cols))
+    column = flat - row * cols
+    return (row - block * rows).astype(F32), column.astype(F32)
+
+
+def sample_line(values, row_ref, col_ref, real_ref, imag_ref, i, rows, cols, count):
+    for start, step in chunks(count):
+        here = (pl.ds(i, 1), pl.ds(start, step))
+        found = jnp.dot(values, one_hot(col_ref[here], cols), preferred_element_type=F32)
+        mask = lax.broadcasted_iota(jnp.int32, (rows, step), 0).astype(F32) == row_ref[here]
+        real = jnp.where(mask, found[:rows] + found[rows : 2 * rows], 0.0)
+        imag = jnp.where(mask, found[2 * rows : 3 * rows] + found[3 * rows :], 0.0)
+        real_ref[here] = jnp.sum(real, 0, keepdims=True)
+        imag_ref[here] = jnp.sum(imag, 0, keepdims=True)
+
+
+def shifted_total(sc, period):
+    total = sc[0]
+    for step in range(1, period + 1):
+        total = total + sc[step]
+    return total
+
+
+def kick(packet_ref, real_ref, imag_ref, fresh, period, count):
+    real = jnp.where(fresh, 0.0, real_ref[...])
+    imag = jnp.where(fresh, 0.0, imag_ref[...])
+    phase = packet_ref[:, :count]
+    energy = packet_ref[:, count : 2 * count]
+    energy = energy - kick_rate * (real * jnp.cos(phase) - imag * jnp.sin(phase))
+    phase = phase + energy
+    emit_real = jnp.cos(phase)
+    emit_imag = -jnp.sin(phase)
+    packet_ref[:, :count] = phase
+    packet_ref[:, count : 2 * count] = energy
+    sums = packet_ref[:, 3 * count :]
+    lane = lax.broadcasted_iota(jnp.int32, sums.shape, 1)
+    sums = jnp.where(lane == 2 * period, jnp.sum(emit_real, 1, keepdims=True), sums)
+    packet_ref[:, 3 * count :] = jnp.where(lane == 2 * period + 1, jnp.sum(emit_imag, 1, keepdims=True), sums)
+    return emit_real, emit_imag
+
+
+def first_kick(plan, field, phase, energy, cells, came, shifts):
+    count, rows, cols, lines = plan.count, plan.rows, plan.cols, plan.per_cut
+
+    def kernel(sc, field_ref, phase_ref, energy_ref, cells_ref, came_ref, *refs):
+        outs = refs[: plan.n_row]
+        packet_ref, row_ref, col_ref, real_ref, imag_ref = refs[plan.n_row :]
+        me, cut = lax.axis_index("row"), lax.axis_index("cuts")
+        parts = (phase_ref[...], energy_ref[...], cells_ref[...].astype(F32))
+        for place, part in enumerate(parts):
+            span = slice(place * count, (place + 1) * count)
+            one = jnp.concatenate([part[1:], came_ref[:1, span]], 0)
+            two = jnp.concatenate([part[2:], came_ref[:2, span]], 0)
+            packet_ref[:, span] = jnp.where(sc[0] == 1, one, two)
+        packet_ref[:, 3 * count :] = jnp.zeros((lines, LANES), F32)
+        row_ref[...], col_ref[...] = split_cells(packet_ref[:, 2 * count : 3 * count], me, rows, cols)
+
+        def line(i, carry):
+            values = jnp.concatenate([*halves(field_ref[0, i]), *halves(field_ref[1, i])], 0)
+            sample_line(values, row_ref, col_ref, real_ref, imag_ref, i, rows, cols, count)
+            return carry
+
+        lax.fori_loop(0, lines, line, 0)
+        place = cut * plan.per_cut + lax.broadcasted_iota(jnp.int32, (lines, count), 0)
+        kick(packet_ref, real_ref, imag_ref, remainder(place + sc[0], plan.slots) < sc[0], 0, count)
+        for d in range(plan.n_row):
+            pair = lax.rem((me ^ d) + plan.n_row * plan.turn - plan.turn, plan.n_row)
+            for h in range(plan.held):
+                outs[d][h : h + 1, :] = packet_ref[pl.ds(pair * plan.held + h, 1), :]
+
+    width = 3 * count + LANES
+    scratch = [pltpu.VMEM((lines, width), F32)] + [pltpu.VMEM((lines, count), F32)] * 4
+    outs = [sds((plan.held, width))] * plan.n_row
+    return vmem_call(kernel, outs, [field, phase, energy, cells, came], shifts, scratch)
+
+
+def gather_packet(plan, pieces):
+    count, lines = plan.count, plan.lines
+
+    def kernel(*refs):
+        packet_out, emit_out = refs[plan.n_row :]
+        me = lax.axis_index("row")
+        for d in range(plan.n_row):
+            for h in range(plan.held):
+                packet_out[pl.ds(h * plan.n_row + (me ^ d), 1), :] = refs[d][h : h + 1, :]
+        phase = packet_out[:, :count]
+        emit_out[:lines] = jnp.cos(phase)
+        emit_out[lines:] = -jnp.sin(phase)
+
+    return vmem_call(kernel, (sds((lines, 3 * count + LANES)), sds((2 * lines, count))), list(pieces))
+
+
+def line_block(plan):
+    return lax.rem(lax.broadcasted_iota(jnp.int32, (plan.lines, plan.count), 0), jnp.int32(plan.n_row))
+
+
+def sample_and_kick(plan, period, grid, own, came, shifts):
+    count, rows, cols, lines, n_row = plan.count, plan.rows, plan.cols, plan.lines, plan.n_row
+    last = period + 1 == plan.periods
+    width = 3 * count + LANES
+
+    def kernel(sc, grid_ref, own_ref, came_ref, packet_out, emit_out, *refs):
+        row_ref, col_ref, real_ref, imag_ref = refs[-4:]
+        me, cut = lax.axis_index("row"), lax.axis_index("cuts")
+        one = jnp.concatenate([own_ref[n_row:], came_ref[:n_row]], 0)
+        two = came_ref[...] if plan.held == KMAX else jnp.concatenate([own_ref[2 * n_row :], came_ref[...]], 0)
+        packet_out[...] = jnp.where(sc[period] == 1, one, two)
+        row_ref[...], col_ref[...] = split_cells(packet_out[:, 2 * count : 3 * count], line_block(plan), rows, cols)
+
+        def line(i, carry):
+            sample_line(grid_ref[i], row_ref, col_ref, real_ref, imag_ref, i, rows, cols, count)
+            return carry
+
+        lax.fori_loop(0, lines, line, 0)
+        slot = cut * plan.per_cut + me * plan.held + lax.div(lax.broadcasted_iota(jnp.int32, (lines, count), 0), jnp.int32(n_row))
+        fresh = remainder(slot - plan.lead + shifted_total(sc, period), plan.slots) < sc[period]
+        emit_real, emit_imag = kick(packet_out, real_ref, imag_ref, fresh, period, count)
+        emit_out[:lines] = emit_real
+        emit_out[lines:] = emit_imag
+        if last:
+            outs = refs[:n_row]
+            for d in range(n_row):
+                for h in range(plan.held):
+                    line_at = pl.ds(h * n_row + (me ^ d), 1)
+                    outs[d][h : h + 1, : 2 * count] = packet_out[line_at, : 2 * count]
+                    sums = packet_out[h * n_row : (h + 1) * n_row, 3 * count :]
+                    outs[d][h : h + 1, 2 * count :] = jnp.sum(sums, 0, keepdims=True)
+
+    outs = [sds((lines, width)), sds((2 * lines, count))]
+    if last:
+        outs += [sds((plan.held, 2 * count + LANES))] * n_row
+    return vmem_call(kernel, outs, [grid, own, came], shifts, [pltpu.VMEM((lines, count), F32)] * 4)
+
+
+def deposit_and_sweep(plan, period, grids, packet, emit, props, shifts):
+    count, rows, cols, lines, n_row, held = plan.count, plan.rows, plan.cols, plan.lines, plan.n_row, plan.held
+    all_rows = n_row * rows
+    first, last = period == 0, period + 1 == plan.periods
+    n_grids = len(grids)
+
+    def kernel(sc, *refs):
+        grid_refs = refs[:n_grids]
+        packet_ref, emit_ref, row_high, row_low, col_high, col_low = refs[n_grids : n_grids + 6]
+        outs = refs[n_grids + 6 : -7]
+        row_ref, col_ref, high_ref, low_ref, mid_high, mid_low, done_ref = refs[-7:]
+        me, cut = lax.axis_index("row"), lax.axis_index("cuts")
+        row_ref[...], col_ref[...] = split_cells(packet_ref[:, 2 * count : 3 * count], line_block(plan), rows, cols)
+
+        def slot(h, carry):
+            index = remainder(cut * plan.per_cut + me * held + h - plan.lead + shifted_total(sc, period), plan.slots)
+            keep = jnp.where(index < sc[period], 0.0, 1.0).astype(F32)
+
+            def line(b, piece):
+                i = h * n_row + b
+                total = jnp.zeros((4 * rows, cols), F32)
+                for start, step in chunks(count):
+                    span = pl.ds(start, step)
+                    pick = one_hot(col_ref[pl.ds(i, 1), span], cols)
+                    level = lax.broadcasted_iota(jnp.int32, (rows, step), 0).astype(BF)
+                    mask = level == jnp.broadcast_to(row_ref[pl.ds(i, 1), span].astype(BF), (rows, step))
+                    weights = []
+                    for part in range(2):
+                        for half in halves(emit_ref[pl.ds(part * lines + i, 1), span]):
+                            weights.append(jnp.where(mask, jnp.broadcast_to(half, (rows, step)), jnp.zeros((), BF)))
+                    total += lax.dot_general(
+                        jnp.concatenate(weights, 0), pick, (((1,), (1,)), ((), ())), preferred_element_type=F32
+                    )
+                for part in range(2):
+                    base = 2 * part * rows
+                    if first:
+                        held_value = grid_refs[piece][part, h]
+                    else:
+                        held_value = grid_refs[0][i, pl.ds(base, rows), :].astype(F32)
+                        held_value += grid_refs[0][i, pl.ds(base + rows, rows), :].astype(F32)
+                    added = total[base : base + rows] + total[base + rows : base + 2 * rows]
+                    high, low = halves(keep * held_value + source_gain * added)
+                    where = (pl.ds(pl.multiple_of(b * rows, rows), rows), pl.ds(part * cols, cols))
+                    high_ref[where] = high
+                    low_ref[where] = low
+
+            if first:
+                for d in range(n_row):
+                    line(me ^ d, d)
+            else:
+                def step_line(b, inner):
+                    line(b, None)
+                    return inner
+
+                lax.fori_loop(0, n_row, step_line, 0)
+            high = high_ref[...]
+            swept = jnp.dot(high, col_high[...], preferred_element_type=F32)
+            swept += jnp.dot(high, col_low[...], preferred_element_type=F32)
+            swept += jnp.dot(low_ref[...], col_high[...], preferred_element_type=F32)
+            for part in range(2):
+                high, low = halves(swept[:, part * cols : (part + 1) * cols])
+                mid_high[pl.ds(part * all_rows, all_rows), :] = high
+                mid_low[pl.ds(part * all_rows, all_rows), :] = low
+            high = mid_high[...]
+            result = jnp.dot(row_high[...], high, preferred_element_type=F32)
+            result += jnp.dot(row_low[...], high, preferred_element_type=F32)
+            result += jnp.dot(row_high[...], mid_low[...], preferred_element_type=F32)
+            if last:
+                done_ref[...] = result
+                for part in range(2):
+                    for d in range(n_row):
+                        from_row = pl.multiple_of(part * all_rows + (me ^ d) * rows, rows)
+                        outs[d][part, h] = done_ref[pl.ds(from_row, rows), :]
+            else:
+                for part in range(2):
+                    for b in range(n_row):
+                        high, low = halves(result[part * all_rows + b * rows : part * all_rows + (b + 1) * rows])
+                        outs[0][h * n_row + b, pl.ds(2 * part * rows, rows), :] = high
+                        outs[0][h * n_row + b, pl.ds((2 * part + 1) * rows, rows), :] = low
+            return carry
+
+        lax.fori_loop(0, held, slot, 0)
+
+    if last:
+        outs = [sds((2, held, rows, cols))] * n_row
+    else:
+        outs = [sds((lines, 4 * rows, cols), BF)]
+    scratch = [
+        pltpu.VMEM((lines, count), F32),
+        pltpu.VMEM((lines, count), F32),
+        pltpu.VMEM((all_rows, 2 * cols), BF),
+        pltpu.VMEM((all_rows, 2 * cols), BF),
+        pltpu.VMEM((2 * all_rows, cols), BF),
+        pltpu.VMEM((2 * all_rows, cols), BF),
+        pltpu.VMEM((2 * all_rows, cols), F32),
+    ]
+    return vmem_call(kernel, outs, [*grids, packet, emit, *props], shifts, scratch)
+
+
+def split_props(row_prop, col_prop):
+    size, cols = row_prop.shape[1], col_prop.shape[1]
+
+    def kernel(row_ref, col_ref, row_high, row_low, col_high, col_low):
+        def put(high_ref, low_ref, top, left, value):
+            where = (slice(top, top + value.shape[0]), slice(left, left + value.shape[1]))
+            high_ref[where], low_ref[where] = halves(value)
+
+        put(row_high, row_low, 0, 0, row_ref[0])
+        put(row_high, row_low, 0, size, -row_ref[1])
+        put(row_high, row_low, size, 0, row_ref[1])
+        put(row_high, row_low, size, size, row_ref[0])
+        real, imag = col_ref[0].T, col_ref[1].T
+        put(col_high, col_low, 0, 0, real)
+        put(col_high, col_low, 0, cols, imag)
+        put(col_high, col_low, cols, 0, -imag)
+        put(col_high, col_low, cols, cols, real)
+
+    outs = [sds((2 * size, 2 * size), BF)] * 2 + [sds((2 * cols, 2 * cols), BF)] * 2
+    return vmem_call(kernel, outs, [row_prop, col_prop])
+
+
+def edges(plan, pieces, axis):
+    shape = list(pieces[0].shape)
+    parts = [(plan.held - plan.ahead, plan.held, plan.n_row - 1), (0, plan.behind, 0)]
+    parts = [part for part in parts if part[1] > part[0]]
+    outs = [sds(tuple(shape[:axis] + [stop - start] + shape[axis + 1 :])) for start, stop, _ in parts]
+
+    def kernel(*refs):
+        me = lax.axis_index("row")
+        for d in range(plan.n_row):
+            for (start, stop, owner), out in zip(parts, refs[plan.n_row :]):
+                @pl.when((me ^ d) == owner)
+                def _(d=d, start=start, stop=stop, out=out):
+                    span = slice(start, stop)
+                    out[...] = refs[d][:, span] if axis else refs[d][span]
+
+    return vmem_call(kernel, outs, pieces)
+
+
+def slipped(plan, pieces, axis):
+    ring = [(c, (c + 1) % plan.n_cuts) for c in range(plan.n_cuts)]
+    kept = edges(plan, pieces, axis)
+    moved = []
+    if plan.ahead:
+        moved.append(lax.ppermute(kept[0], "cuts", ring))
+    if plan.behind:
+        moved.append(lax.ppermute(kept[-1], "cuts", [(b, a) for a, b in ring]))
+    return moved
+
+
+def joined_at(plan, refs, target, put):
+    me = lax.axis_index("row")
+    extra = refs[plan.n_row :]
+    if plan.ahead:
+        for h in range(plan.ahead):
+            put(h, extra[0], h)
+    for d in range(plan.n_row):
+        for h in range(plan.held):
+            put(plan.ahead + (me ^ d) * plan.held + h, refs[d], h)
+    for h in range(plan.behind):
+        put(plan.ahead + plan.per_cut + h, extra[-1], h)
+
+
+def first_index(plan, sc):
+    return plan.ahead - (shifted_total(sc, plan.periods - 1) - plan.lead)
+
+
+def finish_electrons(plan, pieces, moved, shifts):
+    count, per_cut = plan.count, plan.per_cut
+    many = len(pieces) + len(moved)
+
+    def kernel(sc, *refs):
+        phase_out, energy_out, sums_out, all_ref = refs[many:]
+
+        def put(index, ref, h):
+            all_ref[pl.ds(index, 1), :] = ref[h : h + 1, :]
+
+        joined_at(plan, refs[:many], all_ref, put)
+        start = first_index(plan, sc)
+        for j in range(per_cut):
+            line = all_ref[pl.ds(start + j, 1), :]
+            phase_out[j : j + 1, :] = line[:, :count]
+            energy_out[j : j + 1, :] = line[:, count : 2 * count]
+            sums_out[j : j + 1, :] = line[:, 2 * count :]
+
+    outs = [sds((per_cut, count)), sds((per_cut, count)), sds((per_cut, LANES))]
+    scratch = [pltpu.VMEM((per_cut + plan.ahead + plan.behind, 2 * count + LANES), F32)]
+    return vmem_call(kernel, outs, [*pieces, *moved], shifts, scratch)
+
+
+def finish_field(plan, pieces, moved, shifts):
+    parts, _, rows, cols = pieces[0].shape
+    many = len(pieces) + len(moved)
+
+    def kernel(sc, *refs):
+        out, all_ref = refs[many:]
+
+        def put(index, ref, h):
+            for part in range(parts):
+                all_ref[part, index] = ref[part, h]
+
+        joined_at(plan, refs[:many], all_ref, put)
+        start = first_index(plan, sc)
+        for part in range(parts):
+            for j in range(plan.per_cut):
+                out[part, j] = all_ref[part, start + j]
+
+    scratch = [pltpu.VMEM((parts, plan.per_cut + plan.ahead + plan.behind, rows, cols), F32)]
+    return vmem_call(kernel, sds((parts, plan.per_cut, rows, cols)), [*pieces, *moved], shifts, scratch)
+
+
+def whole_slices(plan, field, row_prop, col_prop, phase, energy, cells, shifts):
+    n_cuts, n_row, held, count = plan.n_cuts, plan.n_row, plan.held, plan.count
+    me = lax.axis_index("row").astype(jnp.int32)
+    both = ("cuts", "row")
+    head = jnp.concatenate([phase[:KMAX], energy[:KMAX], cells[:KMAX].astype(F32)], 1)
+    came = lax.ppermute(head, "cuts", [((c + 1) % n_cuts, c) for c in range(n_cuts)])
+    tables = [plan.spread_table(d) for d in range(n_row)]
+    pieces = []
+    for d in range(n_row):
+        pair = lax.rem((me ^ d) + n_row * plan.turn - plan.turn, n_row)
+        pieces.append(lax.ppermute(lax.dynamic_slice_in_dim(field, pair * held, held, 1), both, tables[d]))
+    props = split_props(row_prop, col_prop)
+    packets = first_kick(plan, field, phase, energy, cells, came, shifts)
+    packets = [lax.ppermute(packet, both, table) for packet, table in zip(packets, tables)]
+    packet, emit = gather_packet(plan, packets)
+
+    devices = n_cuts * n_row
+    back = [(source, (source - 1) % devices) for source in range(devices)]
+    rounds = [[(r, r ^ d) for r in range(n_row)] for d in range(n_row)]
+    grids = pieces
+    for period in range(plan.periods):
+        last = period + 1 == plan.periods
+        if period:
+            packet, emit, *homeward = sample_and_kick(plan, period, grids[0], packet, came, shifts)
+        if last:
+            homeward = [value if d == 0 else lax.ppermute(value, "row", rounds[d]) for d, value in enumerate(homeward)]
+            moved = slipped(plan, homeward, 0)
+            phase, energy, sums = finish_electrons(plan, homeward, moved, shifts)
+        else:
+            came = lax.ppermute(packet[: KMAX * n_row], both, back)
+        grids = deposit_and_sweep(plan, period, grids, packet, emit, props, shifts)
+    pieces = [value if d == 0 else lax.ppermute(value, "row", rounds[d]) for d, value in enumerate(grids)]
+    field = finish_field(plan, pieces, slipped(plan, pieces, 1), shifts)
+    bunching = sums[:, : 2 * plan.periods].T.reshape(plan.periods, 2, plan.per_cut) * (count * n_row) ** (-0.5)
+    return field, phase, energy, bunching
+
+
 def solution(mesh):
+    n_cuts, n_row = mesh.shape["cuts"], mesh.shape["row"]
+
+    def body(field, row_prop, col_prop, phase, energy, cells, shifts):
+        plan = Plan(n_cuts, n_row, field, phase, shifts)
+        if plan.fits():
+            return whole_slices(plan, field, row_prop, col_prop, phase, energy, cells, shifts)
+        return row_blocks(field, row_prop, col_prop, phase, energy, cells, shifts)
+
     return jax.shard_map(
-        shards,
+        body,
         mesh=mesh,
         in_specs=(
             P(None, "cuts", "row", None),

time: 402 us -> 115 us (0.29); the launches traced: 395 us -> 115 us
  waiting for transfers between devices: 217 us -> 28.1 us
  matrix products: 125 us -> 0 us
  Pallas kernels: 0 us -> 48.8 us
  starting transfers between devices: 8.34 us -> 33.2 us
  between operations: 19.8 us -> 0.88 us
  other arithmetic: 12.6 us -> 0.03 us
  blocking collectives: 9.15 us -> 0 us
    all_gather x4 -> x0, waiting for transfers between devices: 217 us -> none  [shards(): lax.all_gather(field, 'row', axis=2, tiled=True)]
    dot_general x40 -> x0, matrix products: 125 us -> none  [the longest x4 46.7 us: shards(): jnp.einsum('psrc,sec->psre', field, col_pick, precision=lax.Precision.HIG...]
    pallas_call x0 -> x14, Pallas kernels: none -> 48.8 us  [vmem_call(): pl.pallas_call(kernel, out_shape=outs, in_specs=specs, out_specs=jax.tree...]
    ppermute x4 -> x22, waiting for transfers between devices: 0.01 us -> 28.1 us  [the longest x4 11.9 us: whole_slices(): lax.ppermute(packet, both, table)]
    ppermute x4 -> x22, starting transfers between devices: 7.19 us -> 33.2 us  [the longest x3 8.17 us: whole_slices(): came = lax.ppermute(packet[:KMAX * n_row], both, back)]
    psum x1 -> x0, blocking collectives: 9.15 us -> none  [shards(): partials.append(lax.psum(local_sums, 'row'))]
    another operation x17 -> x0, other arithmetic: 5.46 us -> none  [the longest x4 4.26 us: shards(): jnp.stack([cols_product(col_prop[0], field[0]) - cols_product(col_prop[1]...]
  transfers between devices with their start and end apart: 8 -> 22, of which waited for: 4 -> 11; matrix products, arithmetic and copies ran while one was open for 1% -> 1% of each run, Pallas kernels for 0% -> 18%
where the time goes in v1:
time: 115 us
  Pallas kernels  48.8 us (42%)
  starting transfers between devices  33.2 us (29%)
  waiting for transfers between devices  28.1 us (24%)
  local copies, waits for them, and re-layouts  3.55 us (3%)
    pallas_call x14, Pallas kernels, vmem_call(): pl.pallas_call(kernel, out_shape=outs, in_specs=specs, out_specs=jax.tree...  48.8 us
    ppermute x4, waiting for transfers between devices, whole_slices(): lax.ppermute(packet, both, table)  11.9 us
    ppermute x6, waiting for transfers between devices, whole_slices(): lax.ppermute(value, 'row', rounds[d])  9.82 us
    ppermute x3, starting transfers between devices, whole_slices(): came = lax.ppermute(packet[:KMAX * n_row], both, back)  8.17 us
    ppermute x4, starting transfers between devices, whole_slices(): lax.ppermute(lax.dynamic_slice_in_dim(field, pair * held, held, 1), both,...  7.47 us
    ppermute x2, starting transfers between devices, slipped(): moved.append(lax.ppermute(kept[-1], 'cuts', [(b, a) for a, b in ring]))  5.7 us
    ppermute x1, starting transfers between devices, whole_slices(): lax.ppermute(head, 'cuts', [((c + 1) % n_cuts, c) for c in range(n_cuts)])  4.57 us
    ppermute x6, starting transfers between devices, whole_slices(): lax.ppermute(value, 'row', rounds[d])  4.11 us
  transfers between devices with their start and end apart: 22, of which 11 were waited for; matrix products, arithmetic and copies ran while one was open for 1% of the time, Pallas kernels for 18%

profile of v1, /device:TPU:0, one launch (start us, length us, event | category | flops | bytes accessed | tf_op | source)
XLA Modules:
  0.0 114.6 jit_solution(15404063176486391125)
XLA Ops:
  2.2 4.6 %collective-permute-start.4 = (f32[2,6144]{1,0:T(2,128)S(1)}, f32[2,6144]{1,0:T(2,128)S(1)}, u32[]{:S(2)}, u32[]{:S(2)}) collective-permute-start(f32[2,6144]{1,0:T(2,128)S(1)} %pad_maximum_fusion), channel_id=1, source_target_pairs={{4,0},{8,4},{12,8},{16,12},{20,16},{24,20},{28,24},{0,28},{5,1},{9... | collective-permute-start | bytes 147464 | tf_op jit(solution)/shard_map/ppermute | solution.py:512
  6.8 1.7 %collective-permute-done.4.came_ref = f32[2,6144]{1,0:T(2,128)S(1)} collective-permute-done((f32[2,6144]{1,0:T(2,128)S(1)}, f32[2,6144]{1,0:T(2,128)S(1)}, u32[]{:S(2)}, u32[]{:S(2)}) %collective-permute-start.4) | collective-permute-done | bytes 49184 | tf_op jit(solution)/shard_map/ppermute | solution.py:512
  9.8 4.9 %shard_map.102 = (f32[2,6272]{1,0:T(2,128)S(1)}, f32[2,6272]{1,0:T(2,128)S(1)}, f32[2,6272]{1,0:T(2,128)S(1)}, f32[2,6272]{1,0:T(2,128)S(1)}) custom-call(s32[4]{0:T(128)S(1)} %copy-done.6, f32[2,8,64,256]{3,2,1,0:T(8,128)S(1)} %copy-done, f32[8,2048]{1,0:T(8,128)S(1)} %copy-done.3, f32[8,2048]{1,0:T(8,128)S(1)} %copy-done.4, s32[8,2048]{1,0:T(8,128)S(1)} %copy-done.5, ...), custom_call_target="tpu_custom_call" | custom-call | tf_op jit(solution)/shard_map/pallas_call | solution.py:109
  14.7 1.9 %collective-permute-start.5 = (f32[2,6272]{1,0:T(2,128)S(1)}, f32[2,6272]{1,0:T(2,128)S(1)}, u32[]{:S(2)}, u32[]{:S(2)}) collective-permute-start(f32[2,6272]{1,0:T(2,128)S(1)} %get-tuple-element.35), channel_id=1, source_target_pairs={{0,4},{1,5},{2,6},{3,3},{4,8},{5,9},{6,10},{7,7},{8,12},{9,13},{10... | collective-permute-start | bytes 150536 | tf_op jit(solution)/shard_map/ppermute | solution.py:520
  16.9 3.3 %collective-permute-start = (f32[2,2,64,256]{3,2,1,0:T(8,128)S(1)}, f32[2,2,64,256]{3,2,1,0:T(8,128)S(1)}, u32[]{:S(2)}, u32[]{:S(2)}) collective-permute-start(f32[2,2,64,256]{3,2,1,0:T(8,128)S(1)} %get-tuple-element.69), channel_id=1, source_target_pairs={{0,4},{1,5},{2,6},{3,3},{4,8},{5,9},{6,10},{7,7},{8,12},{9,13},{10... | collective-permute-start | bytes 786440 | tf_op jit(solution)/shard_map/ppermute | solution.py:517
  20.2 1.8 %collective-permute-start.1 = (f32[2,2,64,256]{3,2,1,0:T(8,128)S(1)}, f32[2,2,64,256]{3,2,1,0:T(8,128)S(1)}, u32[]{:S(2)}, u32[]{:S(2)}) collective-permute-start(f32[2,2,64,256]{3,2,1,0:T(8,128)S(1)} %get-tuple-element.68), channel_id=1, source_target_pairs={{0,5},{1,4},{2,3},{3,6},{4,9},{5,8},{6,7},{7,10},{8,13},{9,12},{10... | collective-permute-start | bytes 786440 | tf_op jit(solution)/shard_map/ppermute | solution.py:517
  25.6 11.6 %collective-permute-done.8.refs_3_ = f32[2,6272]{1,0:T(2,128)S(1)} collective-permute-done((f32[2,6272]{1,0:T(2,128)S(1)}, f32[2,6272]{1,0:T(2,128)S(1)}, u32[]{:S(2)}, u32[]{:S(2)}) %collective-permute-start.8) | collective-permute-done | bytes 50208 | tf_op jit(solution)/shard_map/ppermute | solution.py:520
  37.6 3.2 %collective-permute-start.9 = (f32[8,6272]{1,0:T(8,128)S(1)}, f32[8,6272]{1,0:T(8,128)S(1)}, u32[]{:S(2)}, u32[]{:S(2)}) collective-permute-start(f32[8,6272]{1,0:T(8,128)S(1)} %get-tuple-element.39.refs_4_.own_ref), channel_id=1, source_target_pairs={{0,31},{1,0},{2,1},{3,2},{4,3},{5,4},{6,5},{7,6},{8,7},{9,8},{10,9... | collective-permute-start | bytes 602120 | tf_op jit(solution)/shard_map/ppermute | solution.py:536
  41.3 5.4 %shard_map.105.grid_ref.refs_0_ = bf16[8,256,256]{2,1,0:T(8,128)(2,1)S(1)} custom-call(s32[4]{0:T(128)S(1)} %copy-done.6, f32[2,2,64,256]{3,2,1,0:T(8,128)S(1)} %collective-permute-done.refs_0_, f32[2,2,64,256]{3,2,1,0:T(8,128)S(1)} %collective-permute-done.1.refs_1_, f32[2,2,64,256]{3,2,1,0:T(8,128)S(1)} %collective-permute-done.2.refs_2_, ...), custom_call_target="tpu_custom_call" | custom-call | tf_op jit(solution)/shard_map/pallas_call | solution.py:109
  46.7 4.9 %shard_map.106 = (f32[8,6272]{1,0:T(8,128)S(1)}, f32[16,2048]{1,0:T(8,128)S(1)}) custom-call(s32[4]{0:T(128)S(1)} %copy-done.6, bf16[8,256,256]{2,1,0:T(8,128)(2,1)S(1)} %shard_map.105.grid_ref.refs_0_, f32[8,6272]{1,0:T(8,128)S(1)} %get-tuple-element.39.refs_4_.own_ref, f32[8,6272]{1,0:T(8,128)S(1)} %collective-permute-done.9.came_ref), custom_call_target="tpu_custom_call" | custom-call | tf_op jit(solution)/shard_map/pallas_call | solution.py:109
  51.6 2.8 %collective-permute-start.10 = (f32[8,6272]{1,0:T(8,128)S(1)}, f32[8,6272]{1,0:T(8,128)S(1)}, u32[]{:S(2)}, u32[]{:S(2)}) collective-permute-start(f32[8,6272]{1,0:T(8,128)S(1)} %get-tuple-element.45.refs_1_.own_ref), channel_id=1, source_target_pairs={{0,31},{1,0},{2,1},{3,2},{4,3},{5,4},{6,5},{7,6},{8,7},{9,8},{10,9... | collective-permute-start | bytes 602120 | tf_op jit(solution)/shard_map/ppermute | solution.py:536
  54.4 6.7 %shard_map.107.grid_ref.refs_0_ = bf16[8,256,256]{2,1,0:T(8,128)(2,1)S(1)} custom-call(s32[4]{0:T(128)S(1)} %copy-done.6, bf16[8,256,256]{2,1,0:T(8,128)(2,1)S(1)} %shard_map.105.grid_ref.refs_0_, f32[8,6272]{1,0:T(8,128)S(1)} %get-tuple-element.45.refs_1_.own_ref, f32[16,2048]{1,0:T(8,128)S(1)} %get-tuple-element.46.refs_2_, ...), custom_call_target="tpu_custom_call" | custom-call | tf_op jit(solution)/shard_map/pallas_call | solution.py:109
  61.1 4.9 %shard_map.108 = (f32[8,6272]{1,0:T(8,128)S(1)}, f32[16,2048]{1,0:T(8,128)S(1)}) custom-call(s32[4]{0:T(128)S(1)} %copy-done.6, bf16[8,256,256]{2,1,0:T(8,128)(2,1)S(1)} %shard_map.107.grid_ref.refs_0_, f32[8,6272]{1,0:T(8,128)S(1)} %get-tuple-element.45.refs_1_.own_ref, f32[8,6272]{1,0:T(8,128)S(1)} %collective-permute-done.10.came_ref), custom_call_target="tpu_custom_call" | custom-call | tf_op jit(solution)/shard_map/pallas_call | solution.py:109
  65.9 2.2 %collective-permute-start.11 = (f32[8,6272]{1,0:T(8,128)S(1)}, f32[8,6272]{1,0:T(8,128)S(1)}, u32[]{:S(2)}, u32[]{:S(2)}) collective-permute-start(f32[8,6272]{1,0:T(8,128)S(1)} %get-tuple-element.47.refs_1_.own_ref), channel_id=1, source_target_pairs={{0,31},{1,0},{2,1},{3,2},{4,3},{5,4},{6,5},{7,6},{8,7},{9,8},{10,9... | collective-permute-start | bytes 602120 | tf_op jit(solution)/shard_map/ppermute | solution.py:536
  68.1 6.7 %shard_map.109.grid_ref.refs_0_ = bf16[8,256,256]{2,1,0:T(8,128)(2,1)S(1)} custom-call(s32[4]{0:T(128)S(1)} %copy-done.6, bf16[8,256,256]{2,1,0:T(8,128)(2,1)S(1)} %shard_map.107.grid_ref.refs_0_, f32[8,6272]{1,0:T(8,128)S(1)} %get-tuple-element.47.refs_1_.own_ref, f32[16,2048]{1,0:T(8,128)S(1)} %get-tuple-element.48.refs_2_, ...), custom_call_target="tpu_custom_call" | custom-call | tf_op jit(solution)/shard_map/pallas_call | solution.py:109
  74.8 4.9 %shard_map.110 = (f32[8,6272]{1,0:T(8,128)S(1)}, f32[16,2048]{1,0:T(8,128)S(1)}, f32[2,4224]{1,0:T(2,128)S(1)}, f32[2,4224]{1,0:T(2,128)S(1)}, f32[2,4224]{1,0:T(2,128)S(1)}, /*index=5*/f32[2,4224]{1,0:T(2,128)S(1)}) custom-call(s32[4]{0:T(128)S(1)} %copy-done.6, bf16[8,256,256]{2,1,0:T(8,128)(2,1)S(1)} %shard_map.109.grid_ref.refs_0_, ...), custom_call_target="tpu_custom_call" | custom-call | tf_op jit(solution)/shard_map/pallas_call | solution.py:109
  79.7 6.8 %shard_map.111 = (f32[2,2,64,256]{3,2,1,0:T(8,128)S(1)}, f32[2,2,64,256]{3,2,1,0:T(8,128)S(1)}, f32[2,2,64,256]{3,2,1,0:T(8,128)S(1)}, f32[2,2,64,256]{3,2,1,0:T(8,128)S(1)}) custom-call(s32[4]{0:T(128)S(1)} %copy-done.6, bf16[8,256,256]{2,1,0:T(8,128)(2,1)S(1)} %shard_map.109.grid_ref.refs_0_, f32[8,6272]{1,0:T(8,128)S(1)} %get-tuple-element.49.refs_1_, ...), custom_call_target="tpu_custom_call" | custom-call | tf_op jit(solution)/shard_map/pallas_call | solution.py:109
  86.7 3.4 %collective-permute-start.14 = (f32[2,2,64,256]{3,2,1,0:T(8,128)S(1)}, f32[2,2,64,256]{3,2,1,0:T(8,128)S(1)}, u32[]{:S(2)}, u32[]{:S(2)}) collective-permute-start(f32[2,2,64,256]{3,2,1,0:T(8,128)S(1)} %get-tuple-element.54), channel_id=1, source_target_pairs={{0,3},{1,2},{2,1},{3,0},{4,7},{5,6},{6,5},{7,4},{8,11},{9,10},{10,... | collective-permute-start | bytes 786440 | tf_op jit(solution)/shard_map/ppermute | solution.py:538
  90.6 5.1 %collective-permute-done.12.refs_1_ = f32[2,2,64,256]{3,2,1,0:T(8,128)S(1)} collective-permute-done((f32[2,2,64,256]{3,2,1,0:T(8,128)S(1)}, f32[2,2,64,256]{3,2,1,0:T(8,128)S(1)}, u32[]{:S(2)}, u32[]{:S(2)}) %collective-permute-start.12) | collective-permute-done | bytes 262176 | tf_op jit(solution)/shard_map/ppermute | solution.py:538
  95.8 2.9 %collective-permute-done.13.refs_2_ = f32[2,2,64,256]{3,2,1,0:T(8,128)S(1)} collective-permute-done((f32[2,2,64,256]{3,2,1,0:T(8,128)S(1)}, f32[2,2,64,256]{3,2,1,0:T(8,128)S(1)}, u32[]{:S(2)}, u32[]{:S(2)}) %collective-permute-start.13) | collective-permute-done | bytes 262176 | tf_op jit(solution)/shard_map/ppermute | solution.py:538
  100.7 3.5 %collective-permute-start.21 = (f32[1,4224]{1,0:T(1,128)S(1)}, f32[1,4224]{1,0:T(1,128)S(1)}, u32[]{:S(2)}, u32[]{:S(2)}) collective-permute-start(f32[1,4224]{1,0:T(1,128)S(1)} %get-tuple-element.62), channel_id=1, source_target_pairs={{4,0},{8,4},{12,8},{16,12},{20,16},{24,20},{28,24},{0,28},{5,1},{9... | collective-permute-start | bytes 50696 | tf_op jit(solution)/shard_map/ppermute | solution.py:442
  108.2 2.2 %collective-permute-start.16 = (f32[2,1,64,256]{3,2,1,0:T(8,128)S(1)}, f32[2,1,64,256]{3,2,1,0:T(8,128)S(1)}, u32[]{:S(2)}, u32[]{:S(2)}) collective-permute-start(f32[2,1,64,256]{3,2,1,0:T(8,128)S(1)} %get-tuple-element.56), channel_id=1, source_target_pairs={{4,0},{8,4},{12,8},{16,12},{20,16},{24,20},{28,24},{0,28},{5,1},{9... | collective-permute-start | bytes 393224 | tf_op jit(solution)/shard_map/ppermute | solution.py:442
  111.1 1.9 %collective-permute-done.16.refs_5_ = f32[2,1,64,256]{3,2,1,0:T(8,128)S(1)} collective-permute-done((f32[2,1,64,256]{3,2,1,0:T(8,128)S(1)}, f32[2,1,64,256]{3,2,1,0:T(8,128)S(1)}, u32[]{:S(2)}, u32[]{:S(2)}) %collective-permute-start.16) | collective-permute-done | bytes 131104 | tf_op jit(solution)/shard_map/ppermute | solution.py:442
  112.9 1.7 %shard_map.113 = f32[2,8,64,256]{3,2,1,0:T(8,128)} custom-call(s32[4]{0:T(128)S(1)} %copy-done.6, f32[2,2,64,256]{3,2,1,0:T(8,128)S(1)} %get-tuple-element.51.refs_0_, f32[2,2,64,256]{3,2,1,0:T(8,128)S(1)} %collective-permute-done.12.refs_1_, f32[2,2,64,256]{3,2,1,0:T(8,128)S(1)} %collective-permute-done.13.refs_2_, ...), custom_call_target="tpu_custom_call" | custom-call | tf_op jit(solution)/shard_map/pallas_call | solution.py:109
  (57 shorter events, 14.8 us)
Async XLA Ops:
  2.2 6.3 %collective-permute-start.4 = (f32[2,6144]{1,0:T(2,128)S(1)}, f32[2,6144]{1,0:T(2,128)S(1)}, u32[]{:S(2)}, u32[]{:S(2)}) collective-permute-start(f32[2,6144]{1,0:T(2,128)S(1)} %pad_maximum_fusion), channel_id=1, source_target_pairs={{4,0},{8,4},{12,8},{16,12},{20,16},{24,20},{28,24},{0,28},{5,1},{9... | collective-permute-start | bytes 147464 | tf_op jit(solution)/shard_map/ppermute | solution.py:512
  14.7 7.3 %collective-permute-start.5 = (f32[2,6272]{1,0:T(2,128)S(1)}, f32[2,6272]{1,0:T(2,128)S(1)}, u32[]{:S(2)}, u32[]{:S(2)}) collective-permute-start(f32[2,6272]{1,0:T(2,128)S(1)} %get-tuple-element.35), channel_id=1, source_target_pairs={{0,4},{1,5},{2,6},{3,3},{4,8},{5,9},{6,10},{7,7},{8,12},{9,13},{10... | collective-permute-start | bytes 150536 | tf_op jit(solution)/shard_map/ppermute | solution.py:520
  16.6 6.8 %collective-permute-start.6 = (f32[2,6272]{1,0:T(2,128)S(1)}, f32[2,6272]{1,0:T(2,128)S(1)}, u32[]{:S(2)}, u32[]{:S(2)}) collective-permute-start(f32[2,6272]{1,0:T(2,128)S(1)} %get-tuple-element.36), channel_id=1, source_target_pairs={{0,5},{1,4},{2,3},{3,6},{4,9},{5,8},{6,7},{7,10},{8,13},{9,12},{10... | collective-permute-start | bytes 150536 | tf_op jit(solution)/shard_map/ppermute | solution.py:520
  16.7 7.9 %collective-permute-start.7 = (f32[2,6272]{1,0:T(2,128)S(1)}, f32[2,6272]{1,0:T(2,128)S(1)}, u32[]{:S(2)}, u32[]{:S(2)}) collective-permute-start(f32[2,6272]{1,0:T(2,128)S(1)} %get-tuple-element.37), channel_id=1, source_target_pairs={{0,6},{1,3},{2,4},{3,5},{4,10},{5,7},{6,8},{7,9},{8,14},{9,11},{10... | collective-permute-start | bytes 150536 | tf_op jit(solution)/shard_map/ppermute | solution.py:520
  16.7 24.0 %copy-start.1 = (f32[2,256,256]{2,1,0:T(8,128)S(1)}, f32[2,256,256]{2,1,0:T(8,128)}, u32[]{:S(2)}) copy-start(f32[2,256,256]{2,1,0:T(8,128)} %row_ref.1) | copy-start | bytes 1572868
  16.8 24.0 %copy-start.2 = (f32[2,256,256]{2,1,0:T(8,128)S(1)}, f32[2,256,256]{2,1,0:T(8,128)}, u32[]{:S(2)}) copy-start(f32[2,256,256]{2,1,0:T(8,128)} %col_ref.1) | copy-start | bytes 1572868
  16.9 24.4 %collective-permute-start = (f32[2,2,64,256]{3,2,1,0:T(8,128)S(1)}, f32[2,2,64,256]{3,2,1,0:T(8,128)S(1)}, u32[]{:S(2)}, u32[]{:S(2)}) collective-permute-start(f32[2,2,64,256]{3,2,1,0:T(8,128)S(1)} %get-tuple-element.69), channel_id=1, source_target_pairs={{0,4},{1,5},{2,6},{3,3},{4,8},{5,9},{6,10},{7,7},{8,12},{9,13},{10... | collective-permute-start | bytes 786440 | tf_op jit(solution)/shard_map/ppermute | solution.py:517
  20.2 21.1 %collective-permute-start.1 = (f32[2,2,64,256]{3,2,1,0:T(8,128)S(1)}, f32[2,2,64,256]{3,2,1,0:T(8,128)S(1)}, u32[]{:S(2)}, u32[]{:S(2)}) collective-permute-start(f32[2,2,64,256]{3,2,1,0:T(8,128)S(1)} %get-tuple-element.68), channel_id=1, source_target_pairs={{0,5},{1,4},{2,3},{3,6},{4,9},{5,8},{6,7},{7,10},{8,13},{9,12},{10... | collective-permute-start | bytes 786440 | tf_op jit(solution)/shard_map/ppermute | solution.py:517
  22.0 19.3 %collective-permute-start.2 = (f32[2,2,64,256]{3,2,1,0:T(8,128)S(1)}, f32[2,2,64,256]{3,2,1,0:T(8,128)S(1)}, u32[]{:S(2)}, u32[]{:S(2)}) collective-permute-start(f32[2,2,64,256]{3,2,1,0:T(8,128)S(1)} %get-tuple-element.67), channel_id=1, source_target_pairs={{0,6},{1,3},{2,4},{3,5},{4,10},{5,7},{6,8},{7,9},{8,14},{9,11},{10... | collective-permute-start | bytes 786440 | tf_op jit(solution)/shard_map/ppermute | solution.py:517
  23.4 17.9 %collective-permute-start.3 = (f32[2,2,64,256]{3,2,1,0:T(8,128)S(1)}, f32[2,2,64,256]{3,2,1,0:T(8,128)S(1)}, u32[]{:S(2)}, u32[]{:S(2)}) collective-permute-start(f32[2,2,64,256]{3,2,1,0:T(8,128)S(1)} %get-tuple-element.66), channel_id=1, source_target_pairs={{0,3},{1,6},{2,5},{3,4},{4,7},{5,10},{6,9},{7,8},{8,11},{9,14},{10... | collective-permute-start | bytes 786440 | tf_op jit(solution)/shard_map/ppermute | solution.py:517
  24.6 12.7 %collective-permute-start.8 = (f32[2,6272]{1,0:T(2,128)S(1)}, f32[2,6272]{1,0:T(2,128)S(1)}, u32[]{:S(2)}, u32[]{:S(2)}) collective-permute-start(f32[2,6272]{1,0:T(2,128)S(1)} %get-tuple-element.38), channel_id=1, source_target_pairs={{0,3},{1,6},{2,5},{3,4},{4,7},{5,10},{6,9},{7,8},{8,11},{9,14},{10... | collective-permute-start | bytes 150536 | tf_op jit(solution)/shard_map/ppermute | solution.py:520
  37.6 9.1 %collective-permute-start.9 = (f32[8,6272]{1,0:T(8,128)S(1)}, f32[8,6272]{1,0:T(8,128)S(1)}, u32[]{:S(2)}, u32[]{:S(2)}) collective-permute-start(f32[8,6272]{1,0:T(8,128)S(1)} %get-tuple-element.39.refs_4_.own_ref), channel_id=1, source_target_pairs={{0,31},{1,0},{2,1},{3,2},{4,3},{5,4},{6,5},{7,6},{8,7},{9,8},{10,9... | collective-permute-start | bytes 602120 | tf_op jit(solution)/shard_map/ppermute | solution.py:536
  51.6 9.5 %collective-permute-start.10 = (f32[8,6272]{1,0:T(8,128)S(1)}, f32[8,6272]{1,0:T(8,128)S(1)}, u32[]{:S(2)}, u32[]{:S(2)}) collective-permute-start(f32[8,6272]{1,0:T(8,128)S(1)} %get-tuple-element.45.refs_1_.own_ref), channel_id=1, source_target_pairs={{0,31},{1,0},{2,1},{3,2},{4,3},{5,4},{6,5},{7,6},{8,7},{9,8},{10,9... | collective-permute-start | bytes 602120 | tf_op jit(solution)/shard_map/ppermute | solution.py:536
  65.9 8.9 %collective-permute-start.11 = (f32[8,6272]{1,0:T(8,128)S(1)}, f32[8,6272]{1,0:T(8,128)S(1)}, u32[]{:S(2)}, u32[]{:S(2)}) collective-permute-start(f32[8,6272]{1,0:T(8,128)S(1)} %get-tuple-element.47.refs_1_.own_ref), channel_id=1, source_target_pairs={{0,31},{1,0},{2,1},{3,2},{4,3},{5,4},{6,5},{7,6},{8,7},{9,8},{10,9... | collective-permute-start | bytes 602120 | tf_op jit(solution)/shard_map/ppermute | solution.py:536
  86.5 9.2 %collective-permute-start.12 = (f32[2,2,64,256]{3,2,1,0:T(8,128)S(1)}, f32[2,2,64,256]{3,2,1,0:T(8,128)S(1)}, u32[]{:S(2)}, u32[]{:S(2)}) collective-permute-start(f32[2,2,64,256]{3,2,1,0:T(8,128)S(1)} %get-tuple-element.52), channel_id=1, source_target_pairs={{0,1},{1,0},{2,3},{3,2},{4,5},{5,4},{6,7},{7,6},{8,9},{9,8},{10,11... | collective-permute-start | bytes 786440 | tf_op jit(solution)/shard_map/ppermute | solution.py:538
  86.6 12.1 %collective-permute-start.13 = (f32[2,2,64,256]{3,2,1,0:T(8,128)S(1)}, f32[2,2,64,256]{3,2,1,0:T(8,128)S(1)}, u32[]{:S(2)}, u32[]{:S(2)}) collective-permute-start(f32[2,2,64,256]{3,2,1,0:T(8,128)S(1)} %get-tuple-element.53), channel_id=1, source_target_pairs={{0,2},{1,3},{2,0},{3,1},{4,6},{5,7},{6,4},{7,5},{8,10},{9,11},{10,... | collective-permute-start | bytes 786440 | tf_op jit(solution)/shard_map/ppermute | solution.py:538
  86.7 12.0 %collective-permute-start.14 = (f32[2,2,64,256]{3,2,1,0:T(8,128)S(1)}, f32[2,2,64,256]{3,2,1,0:T(8,128)S(1)}, u32[]{:S(2)}, u32[]{:S(2)}) collective-permute-start(f32[2,2,64,256]{3,2,1,0:T(8,128)S(1)} %get-tuple-element.54), channel_id=1, source_target_pairs={{0,3},{1,2},{2,1},{3,0},{4,7},{5,6},{6,5},{7,4},{8,11},{9,10},{10,... | collective-permute-start | bytes 786440 | tf_op jit(solution)/shard_map/ppermute | solution.py:538
  90.1 8.9 %collective-permute-start.17 = (f32[2,4224]{1,0:T(2,128)S(1)}, f32[2,4224]{1,0:T(2,128)S(1)}, u32[]{:S(2)}, u32[]{:S(2)}) collective-permute-start(f32[2,4224]{1,0:T(2,128)S(1)} %get-tuple-element.58), channel_id=1, source_target_pairs={{0,1},{1,0},{2,3},{3,2},{4,5},{5,4},{6,7},{7,6},{8,9},{9,8},{10,11... | collective-permute-start | bytes 101384 | tf_op jit(solution)/shard_map/ppermute | solution.py:532
  90.1 8.9 %collective-permute-start.18 = (f32[2,4224]{1,0:T(2,128)S(1)}, f32[2,4224]{1,0:T(2,128)S(1)}, u32[]{:S(2)}, u32[]{:S(2)}) collective-permute-start(f32[2,4224]{1,0:T(2,128)S(1)} %get-tuple-element.59), channel_id=1, source_target_pairs={{0,2},{1,3},{2,0},{3,1},{4,6},{5,7},{6,4},{7,5},{8,10},{9,11},{10,... | collective-permute-start | bytes 101384 | tf_op jit(solution)/shard_map/ppermute | solution.py:532
  95.7 4.8 %collective-permute-start.19 = (f32[2,4224]{1,0:T(2,128)S(1)}, f32[2,4224]{1,0:T(2,128)S(1)}, u32[]{:S(2)}, u32[]{:S(2)}) collective-permute-start(f32[2,4224]{1,0:T(2,128)S(1)} %get-tuple-element.60), channel_id=1, source_target_pairs={{0,3},{1,2},{2,1},{3,0},{4,7},{5,6},{6,5},{7,4},{8,11},{9,10},{10,... | collective-permute-start | bytes 101384 | tf_op jit(solution)/shard_map/ppermute | solution.py:532
  98.7 14.2 %collective-permute-start.15 = (f32[2,2,64,256]{3,2,1,0:T(8,128)S(1)}, f32[2,2,64,256]{3,2,1,0:T(8,128)S(1)}, u32[]{:S(2)}, u32[]{:S(2)}) collective-permute-start(f32[2,2,64,256]{3,2,1,0:T(8,128)S(1)} %get-tuple-element.55), channel_id=1, source_target_pairs={{0,4},{4,8},{8,12},{12,16},{16,20},{20,24},{24,28},{28,0},{1,5},{5... | collective-permute-start | bytes 786440 | tf_op jit(solution)/shard_map/ppermute | solution.py:440
  100.6 6.3 %collective-permute-start.20 = (f32[2,4224]{1,0:T(2,128)S(1)}, f32[2,4224]{1,0:T(2,128)S(1)}, u32[]{:S(2)}, u32[]{:S(2)}) collective-permute-start(f32[2,4224]{1,0:T(2,128)S(1)} %get-tuple-element.61), channel_id=1, source_target_pairs={{0,4},{4,8},{8,12},{12,16},{16,20},{20,24},{24,28},{28,0},{1,5},{5... | collective-permute-start | bytes 101384 | tf_op jit(solution)/shard_map/ppermute | solution.py:440
  100.7 4.9 %collective-permute-start.21 = (f32[1,4224]{1,0:T(1,128)S(1)}, f32[1,4224]{1,0:T(1,128)S(1)}, u32[]{:S(2)}, u32[]{:S(2)}) collective-permute-start(f32[1,4224]{1,0:T(1,128)S(1)} %get-tuple-element.62), channel_id=1, source_target_pairs={{4,0},{8,4},{12,8},{16,12},{20,16},{24,20},{28,24},{0,28},{5,1},{9... | collective-permute-start | bytes 50696 | tf_op jit(solution)/shard_map/ppermute | solution.py:442
  108.2 4.8 %collective-permute-start.16 = (f32[2,1,64,256]{3,2,1,0:T(8,128)S(1)}, f32[2,1,64,256]{3,2,1,0:T(8,128)S(1)}, u32[]{:S(2)}, u32[]{:S(2)}) collective-permute-start(f32[2,1,64,256]{3,2,1,0:T(8,128)S(1)} %get-tuple-element.56), channel_id=1, source_target_pairs={{4,0},{8,4},{12,8},{16,12},{20,16},{24,20},{28,24},{0,28},{5,1},{9... | collective-permute-start | bytes 393224 | tf_op jit(solution)/shard_map/ppermute | solution.py:442
  (7 other events, 18.0 us)

commit v2 on v0

--- a/solution.py
+++ b/solution.py
@@ -1,15 +1,18 @@
 import jax
 import jax.numpy as jnp
 from jax import lax
+from jax.experimental import pallas as pl
+from jax.experimental.pallas import tpu as pltpu
 from jax.sharding import PartitionSpec as P
 
-ELEC = 8192
-PERIODS = 4
+
 KMAX = 2
-
-
 kick_rate = 0.5
 source_gain = 0.5
+BF = jnp.bfloat16
+F32 = jnp.float32
+LANES = 128
+CHUNK = 512
 
 
 def shifted(value, axis, steps):
@@ -35,7 +38,7 @@
     )
 
 
-def shards(field, row_prop, col_prop, phase, energy, cells, shifts):
+def row_blocks(field, row_prop, col_prop, phase, energy, cells, shifts):
     count = field.shape[1]
     row_count = field.shape[2]
     col_count = field.shape[3]
@@ -51,7 +54,7 @@
     ).astype(jnp.float32)
     own_prop = lax.dynamic_slice_in_dim(row_prop, row_start, row_count, 1)
     partials = []
-    for period in range(PERIODS):
+    for period in range(shifts.shape[0]):
         last_slices = field[:, count - KMAX :]
         arrived = shifted(last_slices, "cuts", 1)
         joined = jnp.concatenate([arrived, field], axis=1)
@@ -78,13 +81,478 @@
         )
         field = complex_rows(own_prop, lax.all_gather(field, "row", axis=2, tiled=True))
     bunching = jnp.stack(partials)
-    bunching = bunching * ELEC ** (-0.5)
+    bunching = bunching * (phase.shape[1] * lax.axis_size("row")) ** (-0.5)
     return (field, phase, energy, bunching)
 
 
+def halves(value):
+    high = value.astype(BF)
+    return high, (value - high.astype(F32)).astype(BF)
+
+
+def one_hot(index, size):
+    shape = (size, index.shape[1])
+    level = lax.broadcasted_iota(jnp.int32, shape, 0).astype(BF)
+    return jnp.where(level == jnp.broadcast_to(index.astype(BF), shape), jnp.ones((), BF), jnp.zeros((), BF))
+
+
+def chunks(length):
+    step = CHUNK if length % CHUNK == 0 else length
+    return [(start, step) for start in range(0, length, step)]
+
+
+def vmem_call(kernel, outs, inputs, shifts=None, scratch=(), out_specs=None):
+    vmem = pl.BlockSpec(memory_space=pltpu.VMEM)
+    specs = [vmem] * len(inputs)
+    if shifts is not None:
+        specs = [pl.BlockSpec(memory_space=pltpu.SMEM)] + specs
+        inputs = [shifts] + list(inputs)
+    return pl.pallas_call(
+        kernel,
+        out_shape=outs,
+        in_specs=specs,
+        out_specs=out_specs or jax.tree.map(lambda _: vmem, outs),
+        scratch_shapes=list(scratch),
+        compiler_params=pltpu.CompilerParams(vmem_limit_bytes=32 * 1024 * 1024),
+    )(*inputs)
+
+
+def sds(shape, dtype=F32):
+    return jax.ShapeDtypeStruct(shape, dtype)
+
+
+def remainder(value, divisor):
+    return lax.rem(value + 4 * divisor, jnp.int32(divisor))
+
+
+def ring_place(row):
+    place, shift = row, 1
+    while shift < 16:
+        place = place ^ (place >> shift)
+        shift *= 2
+    return place
+
+
+def ring_row(place):
+    return place ^ (place >> 1)
+
+
+class Plan:
+    def __init__(self, n_cuts, n_row, field, phase, shifts):
+        self.n_cuts, self.n_row = n_cuts, n_row
+        self.per_cut, self.rows, self.cols = field.shape[1:]
+        self.count = phase.shape[1]
+        self.periods = shifts.shape[0]
+        self.held = max(1, self.per_cut // n_row)
+        self.slots = n_cuts * self.per_cut
+        self.lines = self.held * n_row
+        self.farthest = KMAX * self.periods
+        self.line_rows = self.count // self.cols
+        self.field_rows = 2 * self.rows
+        self.home_rows = self.field_rows + -(-(2 * self.line_rows + 1) // 8) * 8
+
+    def fits(self):
+        n = self.n_row
+        if n & (n - 1) or self.per_cut % n or self.held < KMAX or self.count % self.cols or self.cols % LANES:
+            return False
+        return self.farthest <= self.per_cut
+
+
+def split_cells(cells, block, rows, cols):
+    flat = cells.astype(jnp.int32)
+    row = lax.div(flat, jnp.int32(cols))
+    column = flat - row * cols
+    return (row - block * rows).astype(F32), column.astype(F32)
+
+
+def sample_line(values, row_ref, col_ref, real_ref, imag_ref, i, rows, cols, count):
+    for start, step in chunks(count):
+        here = (pl.ds(i, 1), pl.ds(start, step))
+        found = jnp.dot(values, one_hot(col_ref[here], cols), preferred_element_type=F32)
+        mask = lax.broadcasted_iota(jnp.int32, (rows, step), 0).astype(F32) == row_ref[here]
+        real = jnp.where(mask, found[:rows] + found[rows : 2 * rows], 0.0)
+        imag = jnp.where(mask, found[2 * rows : 3 * rows] + found[3 * rows :], 0.0)
+        real_ref[here] = jnp.sum(real, 0, keepdims=True)
+        imag_ref[here] = jnp.sum(imag, 0, keepdims=True)
+
+
+def shifted_total(sc, period):
+    total = sc[0]
+    for step in range(1, period + 1):
+        total = total + sc[step]
+    return total
+
+
+REDUCED_UP_TO = 8192.0
+
+
+def sine_cosine(angle):
+    rounder = 12582912.0
+    turns = (angle * 0.6366197723675814 + rounder) - rounder
+    rest = angle - turns * 1.5703125
+    rest = rest - turns * 4.837512969970703125e-4
+    rest = rest - turns * 7.54978995489188216e-8
+    square = rest * rest
+    sine = rest + rest * square * (-1.6666654611e-1 + square * (8.3321608736e-3 - square * 1.9515295891e-4))
+    cosine = 4.166664568298827e-2 + square * (-1.388731625493765e-3 + square * 2.443315711809948e-5)
+    cosine = 1.0 - 0.5 * square + square * square * cosine
+    quarter = turns.astype(jnp.int32)
+    odd = (quarter & 1) == 1
+    sine, cosine = jnp.where(odd, cosine, sine), jnp.where(odd, sine, cosine)
+    sine = jnp.where((quarter & 2) == 2, -sine, sine)
+    return sine, jnp.where(((quarter + 1) & 2) == 2, -cosine, cosine)
+
+
+def put_sine_cosine(angle, sine_ref, cosine_ref):
+    sine_ref[...], cosine_ref[...] = sine_cosine(angle)
+
+    @pl.when(jnp.logical_not(jnp.max(jnp.abs(angle)) <= REDUCED_UP_TO))
+    def _():
+        sine_ref[...] = jnp.sin(angle)
+        cosine_ref[...] = jnp.cos(angle)
+
+
+def kick(packet_ref, real_ref, imag_ref, sine_ref, cosine_ref, fresh, period, count):
+    phase = packet_ref[:, :count]
+    put_sine_cosine(phase, sine_ref, cosine_ref)
+    change = kick_rate * (real_ref[...] * cosine_ref[...] - imag_ref[...] * sine_ref[...])
+    energy = packet_ref[:, count : 2 * count] - jnp.where(fresh, 0.0, change)
+    phase = phase + energy
+    packet_ref[:, :count] = phase
+    packet_ref[:, count : 2 * count] = energy
+    put_sine_cosine(phase, sine_ref, cosine_ref)
+    sums = packet_ref[:, 3 * count :]
+    lane = lax.broadcasted_iota(jnp.int32, sums.shape, 1)
+    sums = jnp.where(lane == 2 * period, jnp.sum(cosine_ref[...], 1, keepdims=True), sums)
+    sums = jnp.where(lane == 2 * period + 1, -jnp.sum(sine_ref[...], 1, keepdims=True), sums)
+    packet_ref[:, 3 * count :] = sums
+
+
+def first_kick(plan, field, phase, energy, cells, came, shifts):
+    count, rows, cols, lines = plan.count, plan.rows, plan.cols, plan.per_cut
+
+    def kernel(sc, field_ref, phase_ref, energy_ref, cells_ref, came_ref, *refs):
+        outs = refs[: plan.n_row]
+        total_out, packet_ref, row_ref, col_ref, real_ref, imag_ref, sine_ref, cosine_ref = refs[plan.n_row :]
+        total_out[0] = shifted_total(sc, plan.periods - 1)
+        me, cut = lax.axis_index("row"), lax.axis_index("cuts")
+        parts = (phase_ref[...], energy_ref[...], cells_ref[...].astype(F32))
+        for place, part in enumerate(parts):
+            span = slice(place * count, (place + 1) * count)
+            one = jnp.concatenate([part[1:], came_ref[:1, span]], 0)
+            two = jnp.concatenate([part[2:], came_ref[:2, span]], 0)
+            packet_ref[:, span] = jnp.where(sc[0] == 1, one, two)
+        packet_ref[:, 3 * count :] = jnp.zeros((lines, LANES), F32)
+        row_ref[...], col_ref[...] = split_cells(packet_ref[:, 2 * count : 3 * count], me, rows, cols)
+
+        def line(i, carry):
+            values = jnp.concatenate([*halves(field_ref[0, i]), *halves(field_ref[1, i])], 0)
+            sample_line(values, row_ref, col_ref, real_ref, imag_ref, i, rows, cols, count)
+            return carry
+
+        lax.fori_loop(0, lines, line, 0, unroll=4)
+        place = cut * plan.per_cut + lax.broadcasted_iota(jnp.int32, (lines, count), 0)
+        kick(packet_ref, real_ref, imag_ref, sine_ref, cosine_ref, remainder(place + sc[0], plan.slots) < sc[0], 0, count)
+        for d in range(plan.n_row):
+            for h in range(plan.held):
+                outs[d][h : h + 1, :] = packet_ref[pl.ds(ring_place(me ^ d) * plan.held + h, 1), :]
+
+    width = 3 * count + LANES
+    scratch = [pltpu.VMEM((lines, width), F32)] + [pltpu.VMEM((lines, count), F32)] * 6
+    outs = [sds((plan.held, width))] * plan.n_row + [sds((1,), jnp.int32)]
+    vmem = pl.BlockSpec(memory_space=pltpu.VMEM)
+    smem = pl.BlockSpec(memory_space=pltpu.SMEM)
+    return vmem_call(kernel, outs, [field, phase, energy, cells, came], shifts, scratch, [vmem] * plan.n_row + [smem])
+
+
+def gather_packet(plan, pieces):
+    count, lines = plan.count, plan.lines
+
+    def kernel(*refs):
+        packet_out, cosine_out, sine_out = refs[plan.n_row :]
+        me = lax.axis_index("row")
+        for d in range(plan.n_row):
+            for h in range(plan.held):
+                packet_out[pl.ds(h * plan.n_row + (me ^ d), 1), :] = refs[d][h : h + 1, :]
+        put_sine_cosine(packet_out[:, :count], sine_out, cosine_out)
+
+    return vmem_call(kernel, (sds((lines, 3 * count + LANES)), sds((lines, count)), sds((lines, count))), list(pieces))
+
+
+def line_block(plan):
+    return lax.rem(lax.broadcasted_iota(jnp.int32, (plan.lines, plan.count), 0), jnp.int32(plan.n_row))
+
+
+def sample_and_kick(plan, period, grid, own, came, shifts):
+    count, rows, cols, lines, n_row = plan.count, plan.rows, plan.cols, plan.lines, plan.n_row
+    width = 3 * count + LANES
+
+    def kernel(sc, grid_ref, own_ref, came_ref, packet_out, cosine_out, sine_out, *refs):
+        row_ref, col_ref, real_ref, imag_ref = refs[-4:]
+        me, cut = lax.axis_index("row"), lax.axis_index("cuts")
+        one = jnp.concatenate([own_ref[n_row:], came_ref[:n_row]], 0)
+        two = came_ref[...] if plan.held == KMAX else jnp.concatenate([own_ref[2 * n_row :], came_ref[...]], 0)
+        packet_out[...] = jnp.where(sc[period] == 1, one, two)
+        row_ref[...], col_ref[...] = split_cells(packet_out[:, 2 * count : 3 * count], line_block(plan), rows, cols)
+
+        def line(i, carry):
+            sample_line(grid_ref[i], row_ref, col_ref, real_ref, imag_ref, i, rows, cols, count)
+            return carry
+
+        lax.fori_loop(0, lines, line, 0, unroll=4)
+        slot = cut * plan.per_cut + ring_place(me) * plan.held + lax.div(lax.broadcasted_iota(jnp.int32, (lines, count), 0), jnp.int32(n_row))
+        fresh = remainder(slot + shifted_total(sc, period), plan.slots) < sc[period]
+        kick(packet_out, real_ref, imag_ref, sine_out, cosine_out, fresh, period, count)
+
+    outs = [sds((lines, width)), sds((lines, count)), sds((lines, count))]
+    return vmem_call(kernel, outs, [grid, own, came], shifts, [pltpu.VMEM((lines, count), F32)] * 4)
+
+
+def deposit_and_sweep(plan, period, grids, packet, emit, props, shifts):
+    count, rows, cols, lines, n_row, held = plan.count, plan.rows, plan.cols, plan.lines, plan.n_row, plan.held
+    all_rows = n_row * rows
+    first, last = period == 0, period + 1 == plan.periods
+    n_grids = len(grids)
+
+    def kernel(sc, *refs):
+        grid_refs = refs[:n_grids]
+        packet_ref, cosine_ref, sine_ref, row_both, col_high, col_low = refs[n_grids : n_grids + 6]
+        outs = refs[n_grids + 6 : -6]
+        row_ref, col_ref, halves_ref, mid_high, mid_low, done_ref = refs[-6:]
+        me, cut = lax.axis_index("row"), lax.axis_index("cuts")
+        row_ref[...], col_ref[...] = split_cells(packet_ref[:, 2 * count : 3 * count], line_block(plan), rows, cols)
+        low_from = held * all_rows
+
+        def line(h, b, piece):
+            i = h * n_row + b
+            index = remainder(cut * plan.per_cut + ring_place(me) * held + h + shifted_total(sc, period), plan.slots)
+            keep = jnp.where(index < sc[period], 0.0, 1.0).astype(F32)
+            total = jnp.zeros((4 * rows, cols), F32)
+            for start, step in chunks(count):
+                span = pl.ds(start, step)
+                pick = one_hot(col_ref[pl.ds(i, 1), span], cols)
+                level = lax.broadcasted_iota(jnp.int32, (rows, step), 0).astype(BF)
+                mask = level == jnp.broadcast_to(row_ref[pl.ds(i, 1), span].astype(BF), (rows, step))
+                weights = []
+                for value in (cosine_ref[pl.ds(i, 1), span], -sine_ref[pl.ds(i, 1), span]):
+                    for half in halves(source_gain * value):
+                        weights.append(jnp.where(mask, jnp.broadcast_to(half, (rows, step)), jnp.zeros((), BF)))
+                total += lax.dot_general(
+                    jnp.concatenate(weights, 0), pick, (((1,), (1,)), ((), ())), preferred_element_type=F32
+                )
+            for part in range(2):
+                base = 2 * part * rows
+                if first:
+                    held_value = grid_refs[piece][part, h]
+                else:
+                    held_value = grid_refs[0][i, pl.ds(base, rows), :].astype(F32)
+                    held_value += grid_refs[0][i, pl.ds(base + rows, rows), :].astype(F32)
+                added = total[base : base + rows] + total[base + rows : base + 2 * rows]
+                high, low = halves(keep * held_value + added)
+                at = pl.multiple_of(h * all_rows + b * rows, rows)
+                halves_ref[pl.ds(at, rows), pl.ds(part * cols, cols)] = high
+                halves_ref[pl.ds(low_from + at, rows), pl.ds(part * cols, cols)] = low
+
+        def slot_lines(h, carry):
+            for d in range(n_row):
+                line(h, me ^ d if first else d, d)
+            return carry
+
+        lax.fori_loop(0, held, slot_lines, 0)
+        for part in range(2):
+            span = slice(part * cols, (part + 1) * cols)
+            swept = jnp.dot(halves_ref[...], col_high[:, span], preferred_element_type=F32)
+            rest = jnp.dot(halves_ref[:low_from], col_low[:, span], preferred_element_type=F32)
+            high, low = halves(swept[:low_from] + swept[low_from:] + rest)
+            for h in range(held):
+                mid_high[h, part * all_rows : (part + 1) * all_rows] = high[h * all_rows : (h + 1) * all_rows]
+                mid_low[h, part * all_rows : (part + 1) * all_rows] = low[h * all_rows : (h + 1) * all_rows]
+        both = 2 * all_rows
+        for h in range(held):
+            swept = jnp.dot(row_both[...], mid_high[h], preferred_element_type=F32)
+            result = swept[:both] + swept[both:] + jnp.dot(row_both[:both], mid_low[h], preferred_element_type=F32)
+            if last:
+                done_ref[...] = result
+                for part in range(2):
+                    for d in range(n_row):
+                        from_row = pl.multiple_of(part * all_rows + (me ^ d) * rows, rows)
+                        outs[d][h, part * rows : (part + 1) * rows, :] = done_ref[pl.ds(from_row, rows), :]
+            else:
+                for part in range(2):
+                    for b in range(n_row):
+                        high, low = halves(result[part * all_rows + b * rows : part * all_rows + (b + 1) * rows])
+                        outs[0][h * n_row + b, 2 * part * rows : (2 * part + 1) * rows, :] = high
+                        outs[0][h * n_row + b, (2 * part + 1) * rows : (2 * part + 2) * rows, :] = low
+
+        if last:
+            per_line = plan.line_rows
+            for h in range(held):
+                for d in range(n_row):
+                    out = outs[d].at[h]
+                    for which in range(2):
+                        for t in range(per_line):
+                            at = plan.field_rows + which * per_line + t
+                            from_col = which * count + t * cols
+                            value = packet_ref[pl.ds(h * n_row + (me ^ d), 1), from_col : from_col + cols]
+                            out[at : at + 1, :] = value
+                    at = plan.field_rows + 2 * per_line
+                    out[at:, :] = jnp.zeros((plan.home_rows - at, cols), F32)
+                    sums = packet_ref[h * n_row : (h + 1) * n_row, 3 * count :]
+                    out[at : at + 1, :LANES] = jnp.sum(sums, 0, keepdims=True)
+
+    if last:
+        outs = [sds((held, plan.home_rows, cols))] * n_row
+    else:
+        outs = [sds((lines, 4 * rows, cols), BF)]
+    scratch = [
+        pltpu.VMEM((lines, count), F32),
+        pltpu.VMEM((lines, count), F32),
+        pltpu.VMEM((2 * held * all_rows, 2 * cols), BF),
+        pltpu.VMEM((held, 2 * all_rows, cols), BF),
+        pltpu.VMEM((held, 2 * all_rows, cols), BF),
+        pltpu.VMEM((2 * all_rows, cols), F32),
+    ]
+    return vmem_call(kernel, outs, [*grids, packet, *emit, *props], shifts, scratch)
+
+
+def split_props(row_prop, col_prop):
+    size, cols = row_prop.shape[1], col_prop.shape[1]
+
+    def kernel(row_ref, col_ref, row_both, col_high, col_low):
+        for top, left, value in (
+            (0, 0, row_ref[0]), (0, size, -row_ref[1]), (size, 0, row_ref[1]), (size, size, row_ref[0])
+        ):
+            high, low = halves(value)
+            row_both[top : top + size, left : left + size] = high
+            row_both[2 * size + top : 2 * size + top + size, left : left + size] = low
+        real, imag = col_ref[0].T, col_ref[1].T
+        for top, left, value in ((0, 0, real), (0, cols, imag), (cols, 0, -imag), (cols, cols, real)):
+            where = (slice(top, top + cols), slice(left, left + cols))
+            col_high[where], col_low[where] = halves(value)
+
+    outs = [sds((4 * size, 2 * size), BF)] + [sds((2 * cols, 2 * cols), BF)] * 2
+    return vmem_call(kernel, outs, [row_prop, col_prop])
+
+
+def finish(plan, total, pieces):
+    n_row, per_cut, held, rows, cols = plan.n_row, plan.per_cut, plan.held, plan.rows, plan.cols
+    count, per_line, periods = plan.count, plan.line_rows, plan.periods
+    many = len(pieces)
+    at_once = plan.lines // many
+
+    def kernel(*refs):
+        field_out, phase_out, energy_out, bunching_out, sums_ref, out_sem = refs[many:]
+        me = lax.axis_index("row")
+        leaving = []
+        places = []
+        for at in range(plan.lines):
+            d, h = at // held, at % held
+            source = refs[at // at_once].at[at % at_once]
+            target = lax.rem(ring_place(me ^ d) * held + h + total, jnp.int32(per_cut))
+            places.append((source, target))
+            for part in range(2):
+                part_rows = source.at[pl.ds(part * rows, rows)]
+                leaving.append(pltpu.make_async_copy(part_rows, field_out.at[part, target], out_sem.at[at, part]))
+                leaving[-1].start()
+        for source, target in places:
+            for which, out in enumerate((phase_out, energy_out)):
+                for t in range(per_line):
+                    row = plan.field_rows + which * per_line + t
+                    out[pl.ds(target, 1), t * cols : (t + 1) * cols] = source[row : row + 1, :]
+            row = plan.field_rows + 2 * per_line
+            sums_ref[pl.ds(target, 1), :] = source[row : row + 1, :LANES]
+        turned = sums_ref[...].T * (count * n_row) ** (-0.5)
+        for period in range(periods):
+            bunching_out[period] = turned[2 * period : 2 * period + 2, :]
+        for copy in leaving:
+            copy.wait()
+
+    outs = [
+        sds((2, per_cut, rows, cols)),
+        sds((per_cut, count)),
+        sds((per_cut, count)),
+        sds((periods, 2, per_cut)),
+    ]
+    vmem, anywhere = pl.BlockSpec(memory_space=pltpu.VMEM), pl.BlockSpec(memory_space=pl.ANY)
+    return pl.pallas_call(
+        kernel,
+        out_shape=outs,
+        in_specs=[vmem] * many,
+        out_specs=[anywhere] + [vmem] * 3,
+        scratch_shapes=[
+            pltpu.VMEM((per_cut, LANES), F32),
+            pltpu.SemaphoreType.DMA((plan.lines, 2)),
+        ],
+        compiler_params=pltpu.CompilerParams(vmem_limit_bytes=8 * 1024 * 1024),
+    )(*pieces)
+
+
+def whole_slices(plan, field, row_prop, col_prop, phase, energy, cells, shifts):
+    n_cuts, n_row, held = plan.n_cuts, plan.n_row, plan.held
+    me = lax.axis_index("row").astype(jnp.int32)
+    both = ("cuts", "row")
+    head = jnp.concatenate([phase[:KMAX], energy[:KMAX], cells[:KMAX].astype(F32)], 1)
+    came = lax.ppermute(head, "cuts", [((c + 1) % n_cuts, c) for c in range(n_cuts)])
+    rounds = [[(r, r ^ d) for r in range(n_row)] for d in range(n_row)]
+
+    def to_row(value, d):
+        return value if d == 0 else lax.ppermute(value, "row", rounds[d])
+
+    pieces = [to_row(lax.dynamic_slice_in_dim(field, ring_place(me ^ d) * held, held, 1), d) for d in range(n_row)]
+    props = split_props(row_prop, col_prop)
+    *packets, total = first_kick(plan, field, phase, energy, cells, came, shifts)
+    packets = [to_row(packet, d) for d, packet in enumerate(packets)]
+    packet, *emit = gather_packet(plan, packets)
+
+    ring = [c * n_row + ring_row(m) for c in range(n_cuts) for m in range(n_row)]
+    back = [(device, ring[at - 1]) for at, device in enumerate(ring)]
+    grids = pieces
+    for period in range(plan.periods):
+        if period:
+            packet, cosine, sine = sample_and_kick(plan, period, grids[0], packet, came, shifts)
+            emit = (cosine, sine)
+        if period + 1 < plan.periods:
+            came = lax.ppermute(packet[: KMAX * n_row], both, back)
+        grids = deposit_and_sweep(plan, period, grids, packet, emit, props, shifts)
+
+    def homeward(steps):
+        together = steps % held == 0
+
+        def table(d, h):
+            pairs = []
+            for c in range(n_cuts):
+                for r in range(n_row):
+                    cut = (c + (ring_place(r) * held + h + steps) // plan.per_cut) % n_cuts
+                    pairs.append((c * n_row + r, cut * n_row + (r ^ d)))
+            return pairs
+
+        def send(*values):
+            pieces = []
+            for d, value in enumerate(values):
+                if together:
+                    pieces.append(lax.ppermute(value, both, table(d, 0)))
+                else:
+                    pieces += [lax.ppermute(value[h : h + 1], both, table(d, h)) for h in range(held)]
+            return tuple(finish(plan, steps, pieces))
+
+        return send
+
+    totals = range(plan.periods - 1 + KMAX, KMAX * plan.periods + 1)
+    branch = jnp.clip(total[0] - totals[0], 0, len(totals) - 1)
+    return lax.switch(branch, [homeward(steps) for steps in totals], *grids)
+
+
 def solution(mesh):
+    n_cuts, n_row = mesh.shape["cuts"], mesh.shape["row"]
+
+    def body(field, row_prop, col_prop, phase, energy, cells, shifts):
+        plan = Plan(n_cuts, n_row, field, phase, shifts)
+        if plan.fits():
+            return whole_slices(plan, field, row_prop, col_prop, phase, energy, cells, shifts)
+        return row_blocks(field, row_prop, col_prop, phase, energy, cells, shifts)
+
     return jax.shard_map(
-        shards,
+        body,
         mesh=mesh,
         in_specs=(
             P(None, "cuts", "row", None),

time: 402 us -> 93.2 us (0.23); the launches traced: 395 us -> 93 us
  waiting for transfers between devices: 217 us -> 28.6 us
  matrix products: 125 us -> 0 us
  Pallas kernels: 0 us -> 38.5 us
  between operations: 19.8 us -> 1.6 us
  starting transfers between devices: 8.34 us -> 21.4 us
  other arithmetic: 12.6 us -> 0.87 us
  blocking collectives: 9.15 us -> 0 us
    all_gather x4 -> x0, waiting for transfers between devices: 217 us -> none  [shards(): lax.all_gather(field, 'row', axis=2, tiled=True)]
    dot_general x40 -> x0, matrix products: 125 us -> none  [the longest x4 46.7 us: shards(): jnp.einsum('psrc,sec->psre', field, col_pick, precision=lax.Precision.HIG...]
    pallas_call x0 -> x11, Pallas kernels: none -> 38.5 us  [the longest x10 36.7 us: vmem_call(): pl.pallas_call(kernel, out_shape=outs, in_specs=specs, out_specs=out_spec...]
    ppermute x4 -> x14, waiting for transfers between devices: 0.01 us -> 28.6 us  [the longest x4 17.5 us: send(): pieces.append(lax.ppermute(value, both, table(d, 0)))]
    ppermute x4 -> x14, starting transfers between devices: 7.19 us -> 21.4 us  [the longest x3 8.83 us: whole_slices(): came = lax.ppermute(packet[:KMAX * n_row], both, back)]
    psum x1 -> x0, blocking collectives: 9.15 us -> none  [shards(): partials.append(lax.psum(local_sums, 'row'))]
    another operation x17 -> x0, other arithmetic: 5.46 us -> none  [the longest x4 4.26 us: shards(): jnp.stack([cols_product(col_prop[0], field[0]) - cols_product(col_prop[1]...]
  transfers between devices with their start and end apart: 8 -> 14, of which waited for: 4 -> 7; matrix products, arithmetic and copies ran while one was open for 1% -> 0% of each run, Pallas kernels for 0% -> 17%
where the time goes in v2:
time: 93.2 us; the launch traced here: 93 us
  Pallas kernels  38.5 us (41%)
  waiting for transfers between devices  28.6 us (31%)
  starting transfers between devices  21.4 us (23%)
  local copies, waits for them, and re-layouts  2.06 us (2%)
  between operations  1.6 us (2%)
    pallas_call x10, Pallas kernels, vmem_call(): pl.pallas_call(kernel, out_shape=outs, in_specs=specs, out_specs=out_spec...  36.7 us
    ppermute x4, waiting for transfers between devices, send(): pieces.append(lax.ppermute(value, both, table(d, 0)))  17.5 us
    ppermute x6, waiting for transfers between devices, to_row(): return value if d == 0 else lax.ppermute(value, 'row', rounds[d])  9.32 us
    ppermute x3, starting transfers between devices, whole_slices(): came = lax.ppermute(packet[:KMAX * n_row], both, back)  8.83 us
    ppermute x6, starting transfers between devices, to_row(): return value if d == 0 else lax.ppermute(value, 'row', rounds[d])  7.11 us
    ppermute x1, starting transfers between devices, whole_slices(): lax.ppermute(head, 'cuts', [((c + 1) % n_cuts, c) for c in range(n_cuts)])  4.57 us
  transfers between devices with their start and end apart: 14, of which 7 were waited for; matrix products, arithmetic and copies ran while one was open for 0% of the time, Pallas kernels for 17%

profile of v2, /device:TPU:0, one launch (start us, length us, event | category | flops | bytes accessed | tf_op | source)
XLA Modules:
  0.0 93.0 jit_solution(14770424611384358490)
XLA Ops:
  2.3 4.6 %collective-permute-start.24 = (f32[2,6144]{1,0:T(2,128)S(1)}, f32[2,6144]{1,0:T(2,128)S(1)}, u32[]{:S(2)}, u32[]{:S(2)}) collective-permute-start(f32[2,6144]{1,0:T(2,128)S(1)} %pad_maximum_fusion), channel_id=1, source_target_pairs={{4,0},{8,4},{12,8},{16,12},{20,16},{24,20},{28,24},{0,28},{5,1},{9... | collective-permute-start | bytes 147464 | tf_op jit(solution)/shard_map/ppermute | solution.py:495
  6.8 1.7 %collective-permute-done.24.came_ref = f32[2,6144]{1,0:T(2,128)S(1)} collective-permute-done((f32[2,6144]{1,0:T(2,128)S(1)}, f32[2,6144]{1,0:T(2,128)S(1)}, u32[]{:S(2)}, u32[]{:S(2)}) %collective-permute-start.24) | collective-permute-done | bytes 49184 | tf_op jit(solution)/shard_map/ppermute | solution.py:495
  9.8 4.2 %shard_map.118 = (f32[2,6272]{1,0:T(2,128)S(1)}, f32[2,6272]{1,0:T(2,128)S(1)}, f32[2,6272]{1,0:T(2,128)S(1)}, f32[2,6272]{1,0:T(2,128)S(1)}, s32[1]{0:T(128)}) custom-call(s32[4]{0:T(128)S(1)} %copy-done.6, f32[2,8,64,256]{3,2,1,0:T(8,128)S(1)} %copy-done, f32[8,2048]{1,0:T(8,128)S(1)} %copy-done.3, f32[8,2048]{1,0:T(8,128)S(1)} %copy-done.4, ...), custom_call_target="tpu_custom_call" | custom-call | tf_op jit(solution)/shard_map/pallas_call | solution.py:110
  14.0 1.6 %collective-permute-start.28 = (f32[2,6272]{1,0:T(2,128)S(1)}, f32[2,6272]{1,0:T(2,128)S(1)}, u32[]{:S(2)}, u32[]{:S(2)}) collective-permute-start(f32[2,6272]{1,0:T(2,128)S(1)} %get-tuple-element.74), channel_id=1, source_target_pairs={{0,1},{1,0},{2,3},{3,2},{4,5},{5,4},{6,7},{7,6},{8,9},{9,8},{10,11... | collective-permute-start | bytes 150536 | tf_op jit(solution)/shard_map/ppermute | solution.py:499
  16.3 1.5 %collective-permute-start.26 = (f32[2,2,64,256]{3,2,1,0:T(8,128)S(1)}, f32[2,2,64,256]{3,2,1,0:T(8,128)S(1)}, u32[]{:S(2)}, u32[]{:S(2)}) collective-permute-start(f32[2,2,64,256]{3,2,1,0:T(8,128)S(1)} %get-tuple-element.131), channel_id=1, source_target_pairs={{0,2},{1,3},{2,0},{3,1},{4,6},{5,7},{6,4},{7,5},{8,10},{9,11},{10,... | collective-permute-start | bytes 786440 | tf_op jit(solution)/shard_map/ppermute | solution.py:499
  17.8 1.4 %collective-permute-start.27 = (f32[2,2,64,256]{3,2,1,0:T(8,128)S(1)}, f32[2,2,64,256]{3,2,1,0:T(8,128)S(1)}, u32[]{:S(2)}, u32[]{:S(2)}) collective-permute-start(f32[2,2,64,256]{3,2,1,0:T(8,128)S(1)} %get-tuple-element.128), channel_id=1, source_target_pairs={{0,3},{1,2},{2,1},{3,0},{4,7},{5,6},{6,5},{7,4},{8,11},{9,10},{10,... | collective-permute-start | bytes 786440 | tf_op jit(solution)/shard_map/ppermute | solution.py:499
  19.2 1.5 %collective-permute-start.29 = (f32[2,6272]{1,0:T(2,128)S(1)}, f32[2,6272]{1,0:T(2,128)S(1)}, u32[]{:S(2)}, u32[]{:S(2)}) collective-permute-start(f32[2,6272]{1,0:T(2,128)S(1)} %get-tuple-element.75), channel_id=1, source_target_pairs={{0,2},{1,3},{2,0},{3,1},{4,6},{5,7},{6,4},{7,5},{8,10},{9,11},{10,... | collective-permute-start | bytes 150536 | tf_op jit(solution)/shard_map/ppermute | solution.py:499
  21.2 8.2 %collective-permute-done.29.refs_2_ = f32[2,6272]{1,0:T(2,128)S(1)} collective-permute-done((f32[2,6272]{1,0:T(2,128)S(1)}, f32[2,6272]{1,0:T(2,128)S(1)}, u32[]{:S(2)}, u32[]{:S(2)}) %collective-permute-start.29) | collective-permute-done | bytes 50208 | tf_op jit(solution)/shard_map/ppermute | solution.py:499
  30.8 3.7 %collective-permute-start.31 = (f32[8,6272]{1,0:T(8,128)S(1)}, f32[8,6272]{1,0:T(8,128)S(1)}, u32[]{:S(2)}, u32[]{:S(2)}) collective-permute-start(f32[8,6272]{1,0:T(8,128)S(1)} %get-tuple-element.77.refs_4_.own_ref), channel_id=1, source_target_pairs={{0,30},{1,0},{3,1},{2,3},{4,2},{5,4},{7,5},{6,7},{8,6},{9,8},{11,9... | collective-permute-start | bytes 602120 | tf_op jit(solution)/shard_map/ppermute | solution.py:515
  34.9 5.1 %shard_map.121.grid_ref.refs_0_ = bf16[8,256,256]{2,1,0:T(8,128)(2,1)S(1)} custom-call(s32[4]{0:T(128)S(1)} %copy-done.6, f32[2,2,64,256]{3,2,1,0:T(8,128)S(1)} %get-tuple-element.130.refs_0_, f32[2,2,64,256]{3,2,1,0:T(8,128)S(1)} %collective-permute-done.25.refs_1_, f32[2,2,64,256]{3,2,1,0:T(8,128)S(1)} %collective-permute-done.26.refs_2_, ...), custom_call_target="tpu_custom_call" | custom-call | tf_op jit(solution)/shard_map/pallas_call | solution.py:110
  40.1 3.8 %shard_map.122 = (f32[8,6272]{1,0:T(8,128)S(1)}, f32[8,2048]{1,0:T(8,128)S(1)}, f32[8,2048]{1,0:T(8,128)S(1)}) custom-call(s32[4]{0:T(128)S(1)} %copy-done.6, bf16[8,256,256]{2,1,0:T(8,128)(2,1)S(1)} %shard_map.121.grid_ref.refs_0_, f32[8,6272]{1,0:T(8,128)S(1)} %get-tuple-element.77.refs_4_.own_ref, f32[8,6272]{1,0:T(8,128)S(1)} %collective-permute-done.31.came_ref), custom_call_target="tpu_custom_call" | custom-call | tf_op jit(solution)/shard_map/pallas_call | solution.py:110
  43.8 2.4 %collective-permute-start.32 = (f32[8,6272]{1,0:T(8,128)S(1)}, f32[8,6272]{1,0:T(8,128)S(1)}, u32[]{:S(2)}, u32[]{:S(2)}) collective-permute-start(f32[8,6272]{1,0:T(8,128)S(1)} %get-tuple-element.83.refs_1_.own_ref), channel_id=1, source_target_pairs={{0,30},{1,0},{3,1},{2,3},{4,2},{5,4},{7,5},{6,7},{8,6},{9,8},{11,9... | collective-permute-start | bytes 602120 | tf_op jit(solution)/shard_map/ppermute | solution.py:515
  46.3 5.1 %shard_map.123.grid_ref.refs_0_ = bf16[8,256,256]{2,1,0:T(8,128)(2,1)S(1)} custom-call(s32[4]{0:T(128)S(1)} %copy-done.6, bf16[8,256,256]{2,1,0:T(8,128)(2,1)S(1)} %shard_map.121.grid_ref.refs_0_, f32[8,6272]{1,0:T(8,128)S(1)} %get-tuple-element.83.refs_1_.own_ref, f32[8,2048]{1,0:T(8,128)S(1)} %get-tuple-element.84.refs_2_, ...), custom_call_target="tpu_custom_call" | custom-call | tf_op jit(solution)/shard_map/pallas_call | solution.py:110
  51.4 3.8 %shard_map.124 = (f32[8,6272]{1,0:T(8,128)S(1)}, f32[8,2048]{1,0:T(8,128)S(1)}, f32[8,2048]{1,0:T(8,128)S(1)}) custom-call(s32[4]{0:T(128)S(1)} %copy-done.6, bf16[8,256,256]{2,1,0:T(8,128)(2,1)S(1)} %shard_map.123.grid_ref.refs_0_, f32[8,6272]{1,0:T(8,128)S(1)} %get-tuple-element.83.refs_1_.own_ref, f32[8,6272]{1,0:T(8,128)S(1)} %collective-permute-done.32.came_ref), custom_call_target="tpu_custom_call" | custom-call | tf_op jit(solution)/shard_map/pallas_call | solution.py:110
  55.2 2.7 %collective-permute-start.33 = (f32[8,6272]{1,0:T(8,128)S(1)}, f32[8,6272]{1,0:T(8,128)S(1)}, u32[]{:S(2)}, u32[]{:S(2)}) collective-permute-start(f32[8,6272]{1,0:T(8,128)S(1)} %get-tuple-element.86.refs_1_.own_ref), channel_id=1, source_target_pairs={{0,30},{1,0},{3,1},{2,3},{4,2},{5,4},{7,5},{6,7},{8,6},{9,8},{11,9... | collective-permute-start | bytes 602120 | tf_op jit(solution)/shard_map/ppermute | solution.py:515
  58.5 5.1 %shard_map.125.grid_ref.refs_0_ = bf16[8,256,256]{2,1,0:T(8,128)(2,1)S(1)} custom-call(s32[4]{0:T(128)S(1)} %copy-done.6, bf16[8,256,256]{2,1,0:T(8,128)(2,1)S(1)} %shard_map.123.grid_ref.refs_0_, f32[8,6272]{1,0:T(8,128)S(1)} %get-tuple-element.86.refs_1_.own_ref, f32[8,2048]{1,0:T(8,128)S(1)} %get-tuple-element.87.refs_2_, ...), custom_call_target="tpu_custom_call" | custom-call | tf_op jit(solution)/shard_map/pallas_call | solution.py:110
  63.6 3.7 %shard_map.126 = (f32[8,6272]{1,0:T(8,128)S(1)}, f32[8,2048]{1,0:T(8,128)S(1)}, f32[8,2048]{1,0:T(8,128)S(1)}) custom-call(s32[4]{0:T(128)S(1)} %copy-done.6, bf16[8,256,256]{2,1,0:T(8,128)(2,1)S(1)} %shard_map.125.grid_ref.refs_0_, f32[8,6272]{1,0:T(8,128)S(1)} %get-tuple-element.86.refs_1_.own_ref, f32[8,6272]{1,0:T(8,128)S(1)} %collective-permute-done.33.came_ref), custom_call_target="tpu_custom_call" | custom-call | tf_op jit(solution)/shard_map/pallas_call | solution.py:110
  67.4 5.2 %shard_map.127 = (f32[2,152,256]{2,1,0:T(8,128)S(1)}, f32[2,152,256]{2,1,0:T(8,128)S(1)}, f32[2,152,256]{2,1,0:T(8,128)S(1)}, f32[2,152,256]{2,1,0:T(8,128)S(1)}) custom-call(s32[4]{0:T(128)S(1)} %copy-done.6, bf16[8,256,256]{2,1,0:T(8,128)(2,1)S(1)} %shard_map.125.grid_ref.refs_0_, f32[8,6272]{1,0:T(8,128)S(1)} %get-tuple-element.89.refs_1_, ...), custom_call_target="tpu_custom_call" | custom-call | tf_op jit(solution)/shard_map/pallas_call | solution.py:110
  72.6 20.2 %conditional.1 = ((f32[2,8,64,256]{3,2,1,0:T(8,128)}, f32[8,2048]{1,0:T(8,128)}, f32[8,2048]{1,0:T(8,128)}, f32[4,2,8]{2,1,0:T(2,128)})) conditional(s32[]{:T(128)} %bitcast, (f32[2,152,256]{2,1,0:T(8,128)S(1)}, f32[2,152,256]{2,1,0:T(8,128)S(1)}, f32[2,152,256]{2,1,0:T(8,128)S(1)}, ...), branch_computations={%region_0.1_spmd, %region_1.2_spmd, %region_2.3_spmd, %region_3.4_... | conditional | bytes 7471432 | solution.py:542
  73.5 7.3 %collective-permute-done.4.refs_0_ = f32[2,152,256]{2,1,0:T(8,128)S(1)} collective-permute-done((f32[2,152,256]{2,1,0:T(8,128)S(1)}, f32[2,152,256]{2,1,0:T(8,128)S(1)}, u32[]{:S(2)}, u32[]{:S(2)}) %collective-permute-start.4) | collective-permute-done | bytes 311328 | tf_op jit(solution)/shard_map/cond/branch_3_fun/ppermute | solution.py:533
  80.8 2.2 %collective-permute-done.5.refs_1_ = f32[2,152,256]{2,1,0:T(8,128)S(1)} collective-permute-done((f32[2,152,256]{2,1,0:T(8,128)S(1)}, f32[2,152,256]{2,1,0:T(8,128)S(1)}, u32[]{:S(2)}, u32[]{:S(2)}) %collective-permute-start.5) | collective-permute-done | bytes 311328 | tf_op jit(solution)/shard_map/cond/branch_3_fun/ppermute | solution.py:533
  83.0 5.6 %collective-permute-done.6.refs_2_ = f32[2,152,256]{2,1,0:T(8,128)S(1)} collective-permute-done((f32[2,152,256]{2,1,0:T(8,128)S(1)}, f32[2,152,256]{2,1,0:T(8,128)S(1)}, u32[]{:S(2)}, u32[]{:S(2)}) %collective-permute-start.6) | collective-permute-done | bytes 311328 | tf_op jit(solution)/shard_map/cond/branch_3_fun/ppermute | solution.py:533
  88.6 2.4 %collective-permute-done.7.refs_3_ = f32[2,152,256]{2,1,0:T(8,128)S(1)} collective-permute-done((f32[2,152,256]{2,1,0:T(8,128)S(1)}, f32[2,152,256]{2,1,0:T(8,128)S(1)}, u32[]{:S(2)}, u32[]{:S(2)}) %collective-permute-start.7) | collective-permute-done | bytes 311328 | tf_op jit(solution)/shard_map/cond/branch_3_fun/ppermute | solution.py:533
  91.0 1.8 %branch_3_fun.1 = (f32[2,8,64,256]{3,2,1,0:T(8,128)}, f32[8,2048]{1,0:T(8,128)}, f32[8,2048]{1,0:T(8,128)}, f32[4,2,8]{2,1,0:T(2,128)}) custom-call(f32[2,152,256]{2,1,0:T(8,128)S(1)} %collective-permute-done.4.refs_0_, f32[2,152,256]{2,1,0:T(8,128)S(1)} %collective-permute-done.5.refs_1_, f32[2,152,256]{2,1,0:T(8,128)S(1)} %collective-permute-done.6.refs_2_, ...), custom_call_target="tpu_custom_call" | custom-call | tf_op jit(solution)/shard_map/cond/branch_3_fun/pallas_call | solution.py:477
  (37 shorter events, 6.7 us)
Async XLA Ops:
  1.5 0.7 slice-start
  1.5 0.7 slice-start.1
  2.2 6.4 %copy-start.4 = (f32[8,2048]{1,0:T(8,128)S(1)}, f32[8,2048]{1,0:T(8,128)}, u32[]{:S(2)}) copy-start(f32[8,2048]{1,0:T(8,128)} %energy_ref.1) | copy-start | bytes 196612
  2.2 6.4 %copy-start.5 = (s32[8,2048]{1,0:T(8,128)S(1)}, s32[8,2048]{1,0:T(8,128)}, u32[]{:S(2)}) copy-start(s32[8,2048]{1,0:T(8,128)} %cells_ref.1) | copy-start | bytes 196612
  2.2 6.3 %copy-start.3 = (f32[8,2048]{1,0:T(8,128)S(1)}, f32[8,2048]{1,0:T(8,128)}, u32[]{:S(2)}) copy-start(f32[8,2048]{1,0:T(8,128)} %phase_ref.1) | copy-start | bytes 196612
  2.3 6.3 %collective-permute-start.24 = (f32[2,6144]{1,0:T(2,128)S(1)}, f32[2,6144]{1,0:T(2,128)S(1)}, u32[]{:S(2)}, u32[]{:S(2)}) collective-permute-start(f32[2,6144]{1,0:T(2,128)S(1)} %pad_maximum_fusion), channel_id=1, source_target_pairs={{4,0},{8,4},{12,8},{16,12},{20,16},{24,20},{28,24},{0,28},{5,1},{9... | collective-permute-start | bytes 147464 | tf_op jit(solution)/shard_map/ppermute | solution.py:495
  6.8 1.8 %copy-start.6 = (s32[4]{0:T(128)S(1)}, s32[4]{0:T(128)}, u32[]{:S(2)}) copy-start(s32[4]{0:T(128)} %sc.15) | copy-start | bytes 52
  8.6 1.2 %copy-start = (f32[2,8,64,256]{3,2,1,0:T(8,128)S(1)}, f32[2,8,64,256]{3,2,1,0:T(8,128)}, u32[]{:S(2)}) copy-start(f32[2,8,64,256]{3,2,1,0:T(8,128)} %field_ref.1) | copy-start | bytes 3145732
  14.0 6.7 %collective-permute-start.28 = (f32[2,6272]{1,0:T(2,128)S(1)}, f32[2,6272]{1,0:T(2,128)S(1)}, u32[]{:S(2)}, u32[]{:S(2)}) collective-permute-start(f32[2,6272]{1,0:T(2,128)S(1)} %get-tuple-element.74), channel_id=1, source_target_pairs={{0,1},{1,0},{2,3},{3,2},{4,5},{5,4},{6,7},{7,6},{8,9},{9,8},{10,11... | collective-permute-start | bytes 150536 | tf_op jit(solution)/shard_map/ppermute | solution.py:499
  15.6 19.0 %copy-start.1 = (f32[2,256,256]{2,1,0:T(8,128)S(1)}, f32[2,256,256]{2,1,0:T(8,128)}, u32[]{:S(2)}) copy-start(f32[2,256,256]{2,1,0:T(8,128)} %row_ref.1) | copy-start | bytes 1572868
  15.6 19.0 %copy-start.2 = (f32[2,256,256]{2,1,0:T(8,128)S(1)}, f32[2,256,256]{2,1,0:T(8,128)}, u32[]{:S(2)}) copy-start(f32[2,256,256]{2,1,0:T(8,128)} %col_ref.1) | copy-start | bytes 1572868
  15.7 19.3 %collective-permute-start.25 = (f32[2,2,64,256]{3,2,1,0:T(8,128)S(1)}, f32[2,2,64,256]{3,2,1,0:T(8,128)S(1)}, u32[]{:S(2)}, u32[]{:S(2)}) collective-permute-start(f32[2,2,64,256]{3,2,1,0:T(8,128)S(1)} %get-tuple-element.129), channel_id=1, source_target_pairs={{0,1},{1,0},{2,3},{3,2},{4,5},{5,4},{6,7},{7,6},{8,9},{9,8},{10,11... | collective-permute-start | bytes 786440 | tf_op jit(solution)/shard_map/ppermute | solution.py:499
  16.3 18.7 %collective-permute-start.26 = (f32[2,2,64,256]{3,2,1,0:T(8,128)S(1)}, f32[2,2,64,256]{3,2,1,0:T(8,128)S(1)}, u32[]{:S(2)}, u32[]{:S(2)}) collective-permute-start(f32[2,2,64,256]{3,2,1,0:T(8,128)S(1)} %get-tuple-element.131), channel_id=1, source_target_pairs={{0,2},{1,3},{2,0},{3,1},{4,6},{5,7},{6,4},{7,5},{8,10},{9,11},{10,... | collective-permute-start | bytes 786440 | tf_op jit(solution)/shard_map/ppermute | solution.py:499
  17.8 17.2 %collective-permute-start.27 = (f32[2,2,64,256]{3,2,1,0:T(8,128)S(1)}, f32[2,2,64,256]{3,2,1,0:T(8,128)S(1)}, u32[]{:S(2)}, u32[]{:S(2)}) collective-permute-start(f32[2,2,64,256]{3,2,1,0:T(8,128)S(1)} %get-tuple-element.128), channel_id=1, source_target_pairs={{0,3},{1,2},{2,1},{3,0},{4,7},{5,6},{6,5},{7,4},{8,11},{9,10},{10,... | collective-permute-start | bytes 786440 | tf_op jit(solution)/shard_map/ppermute | solution.py:499
  19.2 10.2 %collective-permute-start.29 = (f32[2,6272]{1,0:T(2,128)S(1)}, f32[2,6272]{1,0:T(2,128)S(1)}, u32[]{:S(2)}, u32[]{:S(2)}) collective-permute-start(f32[2,6272]{1,0:T(2,128)S(1)} %get-tuple-element.75), channel_id=1, source_target_pairs={{0,2},{1,3},{2,0},{3,1},{4,6},{5,7},{6,4},{7,5},{8,10},{9,11},{10,... | collective-permute-start | bytes 150536 | tf_op jit(solution)/shard_map/ppermute | solution.py:499
  20.7 9.8 %collective-permute-start.30 = (f32[2,6272]{1,0:T(2,128)S(1)}, f32[2,6272]{1,0:T(2,128)S(1)}, u32[]{:S(2)}, u32[]{:S(2)}) collective-permute-start(f32[2,6272]{1,0:T(2,128)S(1)} %get-tuple-element.76), channel_id=1, source_target_pairs={{0,3},{1,2},{2,1},{3,0},{4,7},{5,6},{6,5},{7,4},{8,11},{9,10},{10,... | collective-permute-start | bytes 150536 | tf_op jit(solution)/shard_map/ppermute | solution.py:499
  30.8 9.3 %collective-permute-start.31 = (f32[8,6272]{1,0:T(8,128)S(1)}, f32[8,6272]{1,0:T(8,128)S(1)}, u32[]{:S(2)}, u32[]{:S(2)}) collective-permute-start(f32[8,6272]{1,0:T(8,128)S(1)} %get-tuple-element.77.refs_4_.own_ref), channel_id=1, source_target_pairs={{0,30},{1,0},{3,1},{2,3},{4,2},{5,4},{7,5},{6,7},{8,6},{9,8},{11,9... | collective-permute-start | bytes 602120 | tf_op jit(solution)/shard_map/ppermute | solution.py:515
  43.8 7.6 %collective-permute-start.32 = (f32[8,6272]{1,0:T(8,128)S(1)}, f32[8,6272]{1,0:T(8,128)S(1)}, u32[]{:S(2)}, u32[]{:S(2)}) collective-permute-start(f32[8,6272]{1,0:T(8,128)S(1)} %get-tuple-element.83.refs_1_.own_ref), channel_id=1, source_target_pairs={{0,30},{1,0},{3,1},{2,3},{4,2},{5,4},{7,5},{6,7},{8,6},{9,8},{11,9... | collective-permute-start | bytes 602120 | tf_op jit(solution)/shard_map/ppermute | solution.py:515
  55.2 8.5 %collective-permute-start.33 = (f32[8,6272]{1,0:T(8,128)S(1)}, f32[8,6272]{1,0:T(8,128)S(1)}, u32[]{:S(2)}, u32[]{:S(2)}) collective-permute-start(f32[8,6272]{1,0:T(8,128)S(1)} %get-tuple-element.86.refs_1_.own_ref), channel_id=1, source_target_pairs={{0,30},{1,0},{3,1},{2,3},{4,2},{5,4},{7,5},{6,7},{8,6},{9,8},{11,9... | collective-permute-start | bytes 602120 | tf_op jit(solution)/shard_map/ppermute | solution.py:515
  72.7 8.2 %collective-permute-start.4 = (f32[2,152,256]{2,1,0:T(8,128)S(1)}, f32[2,152,256]{2,1,0:T(8,128)S(1)}, u32[]{:S(2)}, u32[]{:S(2)}) collective-permute-start(f32[2,152,256]{2,1,0:T(8,128)S(1)} %get-tuple-element.44), channel_id=1, source_target_pairs={{0,4},{1,5},{2,6},{3,7},{4,8},{5,9},{6,10},{7,11},{8,12},{9,13},{1... | collective-permute-start | bytes 933896 | tf_op jit(solution)/shard_map/cond/branch_3_fun/ppermute | solution.py:533
  72.7 10.3 %collective-permute-start.5 = (f32[2,152,256]{2,1,0:T(8,128)S(1)}, f32[2,152,256]{2,1,0:T(8,128)S(1)}, u32[]{:S(2)}, u32[]{:S(2)}) collective-permute-start(f32[2,152,256]{2,1,0:T(8,128)S(1)} %get-tuple-element.45), channel_id=1, source_target_pairs={{0,5},{1,4},{2,7},{3,6},{4,9},{5,8},{6,11},{7,10},{8,13},{9,12},{1... | collective-permute-start | bytes 933896 | tf_op jit(solution)/shard_map/cond/branch_3_fun/ppermute | solution.py:533
  72.8 15.8 %collective-permute-start.6 = (f32[2,152,256]{2,1,0:T(8,128)S(1)}, f32[2,152,256]{2,1,0:T(8,128)S(1)}, u32[]{:S(2)}, u32[]{:S(2)}) collective-permute-start(f32[2,152,256]{2,1,0:T(8,128)S(1)} %get-tuple-element.46), channel_id=1, source_target_pairs={{0,6},{1,7},{2,4},{3,5},{4,10},{5,11},{6,8},{7,9},{8,14},{9,15},{1... | collective-permute-start | bytes 933896 | tf_op jit(solution)/shard_map/cond/branch_3_fun/ppermute | solution.py:533
  72.9 18.2 %collective-permute-start.7 = (f32[2,152,256]{2,1,0:T(8,128)S(1)}, f32[2,152,256]{2,1,0:T(8,128)S(1)}, u32[]{:S(2)}, u32[]{:S(2)}) collective-permute-start(f32[2,152,256]{2,1,0:T(8,128)S(1)} %get-tuple-element.47), channel_id=1, source_target_pairs={{0,7},{1,6},{2,5},{3,4},{4,11},{5,10},{6,9},{7,8},{8,15},{9,14},{1... | collective-permute-start | bytes 933896 | tf_op jit(solution)/shard_map/cond/branch_3_fun/ppermute | solution.py:533
